TPU v7x, 32 devices: a whole 2x2x4 slice. The times are simulated.
32 devices in a mesh: dp: 8 (over y, x, core), mp: 4 (over z).
Axes of the slice: x: 2, y: 2, z: 4, core: 2. Of those that a mesh axis runs over, the one named last changes fastest.
Arguments:
- tokens: bfloat16 [16384, 768], P(('dp', 'mp')), may hold values from -6 to 6
- timesteps: int32 [16], P('dp'), may hold values from 0 to 999
- masked: int32 [16384], P(('dp', 'mp')), may hold values from 0 to 1, as said below
- cotangent: bfloat16 [16384, 768], P(('dp', 'mp')), may hold values from -6 to 6
- step_table: bfloat16 [1000, 768], replicated, may hold values from -3 to 3
- qkv_weight: bfloat16 [768, 3, 768], P(None, None, 'mp'), may hold values from -0.21875 to 0.21875
- qv_bias: float32 [2, 768], P(None, 'mp'), may hold values from -0.6 to 0.6
- out_weight: bfloat16 [768, 768], P('mp'), may hold values from -3.5 to 3.5
- out_bias: float32 [768], replicated, may hold values from -1.8 to 1.8
- first_gain: float32 [768], replicated, may hold values from 0.5 to 1.5
- first_shift: float32 [768], replicated, may hold values from -0.6 to 0.6
- second_gain: float32 [768], replicated, may hold values from 0.5 to 1.5
- second_shift: float32 [768], replicated, may hold values from -0.6 to 0.6
- in_weight: bfloat16 [768, 3072], P(None, 'mp'), may hold values from -0.21875 to 0.21875
- in_bias: bfloat16 [3072], P('mp'), may hold values from -1.796875 to 1.796875
- back_weight: bfloat16 [3072, 768], P('mp'), may hold values from -0.109375 to 0.109375
- back_bias: float32 [768], replicated, may hold values from -1.8 to 1.8
Outputs:
- output: bfloat16 [16384, 768], P(('dp', 'mp'))
- input_grad: float32 [16384, 768], P(('dp', 'mp'))
- table_grad: float32 [1000, 768], replicated
- qkv_weight_grad: float32 [768, 3, 768], P(None, None, 'mp')
- qv_bias_grad: float32 [2, 768], P(None, 'mp')
- out_weight_grad: float32 [768, 768], P('mp')
- out_bias_grad: float32 [768], replicated
- first_gain_grad: float32 [768], replicated
- first_shift_grad: float32 [768], replicated
- second_gain_grad: float32 [768], replicated
- second_shift_grad: float32 [768], replicated
- in_weight_grad: float32 [768, 3072], P(None, 'mp')
- in_bias_grad: float32 [3072], P('mp')
- back_weight_grad: float32 [3072, 768], P('mp')
- back_bias_grad: float32 [768], replicated
Inputs may be any that keep to these rules, and one draw needn't show every extreme that they name: 1 marks a masked token; all tokens of one sequence share one chance of being masked.
All inputs are finite; a program needn't handle non-finite values.
Results may differ from a plain program's by a relative error of at most 0.012.
The roundings to bfloat16 on the way count: a program that leaves them out, or rounds other values in their place, can miss the bound.
Values may be sent and summed in bfloat16 or wider, within the bound.
A program may use at most 128 MiB of HBM per device.

v0:
```python
import jax
import jax.numpy as jnp
from jax import lax
from jax.sharding import PartitionSpec as P

HEAD_DIM = 64
NSTEPS = 1000
L = 1024


EPSILON = 1e-05
HIGHEST = lax.Precision.HIGHEST


def norm_parts(values):
    center = values - jnp.mean(values, axis=-1, keepdims=True)
    inverse = lax.rsqrt(jnp.mean(center * center, axis=-1, keepdims=True) + EPSILON)
    return (center * inverse, inverse)


def norm_back(upstream, normal, inverse):
    return inverse * (
        upstream
        - jnp.mean(upstream, axis=-1, keepdims=True)
        - normal * jnp.mean(upstream * normal, axis=-1, keepdims=True)
    )


def contract_rows(left, right):
    return lax.dot_general(
        left, right, (((0,), (0,)), ((), ())), preferred_element_type=jnp.float32
    )


def contract_cols(left, right):
    return lax.dot_general(
        left, right, (((1,), (1,)), ((), ())), preferred_element_type=jnp.float32
    )


def attend_block(query_block, key_heads, value_heads):
    scores = jnp.einsum(
        "qhc,khc->hqk", query_block, key_heads, preferred_element_type=jnp.float32
    ) * HEAD_DIM ** (-0.5)
    peak = jnp.max(scores, axis=-1, keepdims=True)
    exponent = jnp.exp(scores - peak)
    totals = jnp.sum(exponent, axis=-1, keepdims=True)
    low_probs = (exponent / totals).astype(jnp.bfloat16)
    result = jnp.einsum("hqk,khc->qhc", low_probs, value_heads, preferred_element_type=jnp.float32)
    return (result.astype(jnp.bfloat16), peak[..., 0] + jnp.log(totals[..., 0]))


def attend_sequence(packed):
    query_heads = packed[:, 0]
    key_heads = packed[:, 1]
    value_heads = packed[:, 2]
    seq_len, head_count, head_size = query_heads.shape
    block = min(512, seq_len)
    query_blocks = query_heads.reshape(seq_len // block, block, head_count, head_size)
    outputs, logsum = lax.map(
        lambda query_block: attend_block(query_block, key_heads, value_heads), query_blocks
    )
    return (outputs.reshape(seq_len, head_count * head_size), logsum)


def attend_back(pieces):
    packed, grad_heads, logsum = pieces
    query_heads = packed[:, 0]
    key_heads = packed[:, 1]
    value_heads = packed[:, 2]
    seq_len, head_count, head_size = query_heads.shape
    block = min(512, seq_len)
    query_blocks = query_heads.reshape(seq_len // block, block, head_count, head_size)
    grad_blocks = grad_heads.reshape(seq_len // block, block, head_count, head_size)
    score_scale = HEAD_DIM ** (-0.5)

    def block_step(carry, inputs_block):
        query_block, grad_block, lse_block = inputs_block
        scores = (
            jnp.einsum("qhc,khc->hqk", query_block, key_heads, preferred_element_type=jnp.float32)
            * score_scale
        )
        probs_full = jnp.exp(scores - lse_block[..., None])
        dprobs = jnp.einsum(
            "qhc,khc->hqk", grad_block, value_heads, preferred_element_type=jnp.float32
        )
        inner_sum = jnp.sum(dprobs * probs_full, axis=-1, keepdims=True)
        dscores = (probs_full * (dprobs - inner_sum)).astype(jnp.bfloat16)
        dquery = (
            jnp.einsum("hqk,khc->qhc", dscores, key_heads, preferred_element_type=jnp.float32)
            * score_scale
        )
        key_grad = (
            carry[0]
            + jnp.einsum("hqk,qhc->khc", dscores, query_block, preferred_element_type=jnp.float32)
            * score_scale
        )
        dvalue = carry[1] + jnp.einsum(
            "hqk,qhc->khc",
            probs_full.astype(jnp.bfloat16),
            grad_block,
            preferred_element_type=jnp.float32,
        )
        return ((key_grad, dvalue), dquery)

    zeros_kv = jnp.zeros((seq_len, head_count, head_size), jnp.float32)
    (key_grad, value_grad), query_grad = lax.scan(
        block_step, (zeros_kv, zeros_kv), (query_blocks, grad_blocks, logsum)
    )
    query_grad = query_grad.reshape(seq_len, head_count, head_size)
    return jnp.stack([query_grad, key_grad, value_grad], axis=1).astype(jnp.bfloat16)


def shards(
    tokens,
    timesteps,
    masked,
    cotangent,
    step_table,
    qkv_weight,
    qv_bias,
    out_weight,
    out_bias,
    first_gain,
    first_shift,
    second_gain,
    second_shift,
    in_weight,
    in_bias,
    back_weight,
    back_bias,
):
    local_rows = tokens.shape[0]
    group_rows = local_rows * lax.axis_size("mp")
    seq_count = timesteps.shape[0]
    head_cols = qkv_weight.shape[2]
    first_row = lax.axis_index("mp") * local_rows
    row_seq = (first_row + jnp.arange(local_rows, dtype=jnp.int32)) // L
    select = (row_seq[:, None] == jnp.arange(seq_count, dtype=jnp.int32)[None, :]).astype(
        jnp.float32
    )
    lookup = (timesteps[:, None] == jnp.arange(NSTEPS, dtype=jnp.int32)[None, :]).astype(
        jnp.bfloat16
    )
    seq_rows = jnp.dot(lookup, step_table, preferred_element_type=jnp.float32)
    stream = tokens.astype(jnp.float32) + jnp.dot(select, seq_rows, precision=HIGHEST)
    first_hat, first_inv = norm_parts(stream)
    normed_one = (first_hat * first_gain + first_shift).astype(jnp.bfloat16)
    first_all = lax.all_gather(normed_one, "mp", axis=0, tiled=True)
    qkv_bias = jnp.stack([qv_bias[0], jnp.zeros_like(qv_bias[0]), qv_bias[1]])
    projected = (
        jnp.einsum("rd,djc->rjc", first_all, qkv_weight, preferred_element_type=jnp.float32)
        + qkv_bias
    ).astype(jnp.bfloat16)
    packed = projected.reshape(seq_count, L, 3, head_cols // HEAD_DIM, HEAD_DIM)
    attended, logsum = lax.map(attend_sequence, packed)
    attended = attended.reshape(group_rows, head_cols)
    branch = lax.psum_scatter(
        jnp.dot(attended, out_weight, preferred_element_type=jnp.float32),
        "mp",
        scatter_dimension=0,
        tiled=True,
    )
    mid_stream = stream + (branch + out_bias)
    second_hat, second_inv = norm_parts(mid_stream)
    normed_two = (second_hat * second_gain + second_shift).astype(jnp.bfloat16)
    grad_low = (cotangent.astype(jnp.float32) * masked.astype(jnp.float32)[:, None]).astype(
        jnp.bfloat16
    )
    grad_out = grad_low.astype(jnp.float32)
    second_all = lax.all_gather(normed_two, "mp", axis=0, tiled=True)
    preact = jnp.dot(second_all, in_weight, preferred_element_type=jnp.float32) + in_bias.astype(
        jnp.float32
    )
    active = jax.nn.gelu(preact).astype(jnp.bfloat16)
    feed_out = lax.psum_scatter(
        jnp.dot(active, back_weight, preferred_element_type=jnp.float32),
        "mp",
        scatter_dimension=0,
        tiled=True,
    )
    grad_all = lax.all_gather(grad_low, "mp", axis=0, tiled=True)
    back_weight_grad = contract_rows(active, grad_all)
    pullback = jax.vjp(jax.nn.gelu, preact)[1]
    pre_grad = pullback(contract_cols(grad_all, back_weight))[0].astype(jnp.bfloat16)
    in_bias_grad = jnp.sum(pre_grad.astype(jnp.float32), axis=0)
    in_weight_grad = contract_rows(second_all, pre_grad)
    second_grad = lax.psum_scatter(
        contract_cols(pre_grad, in_weight), "mp", scatter_dimension=0, tiled=True
    )
    output = (mid_stream + (feed_out + back_bias)).astype(jnp.bfloat16)
    back_bias_grad = jnp.sum(grad_out, axis=0)
    second_gain_grad = jnp.sum(second_grad * second_hat, axis=0)
    second_shift_grad = jnp.sum(second_grad, axis=0)
    mid_grad = grad_out + norm_back(second_grad * second_gain, second_hat, second_inv)
    branch_low = mid_grad.astype(jnp.bfloat16)
    out_bias_grad = jnp.sum(branch_low.astype(jnp.float32), axis=0)
    branch_all = lax.all_gather(branch_low, "mp", axis=0, tiled=True)
    out_weight_grad = contract_rows(attended, branch_all)
    attended_grad = (
        contract_cols(branch_all, out_weight)
        .astype(jnp.bfloat16)
        .reshape(seq_count, L, head_cols // HEAD_DIM, HEAD_DIM)
    )
    qkv_grad = lax.map(attend_back, (packed, attended_grad, logsum)).reshape(
        group_rows, 3, head_cols
    )
    qkv_weight_grad = jnp.einsum(
        "rd,rjc->djc", first_all, qkv_grad, preferred_element_type=jnp.float32
    )
    col_sums = jnp.sum(qkv_grad.astype(jnp.float32), axis=0)
    qv_bias_grad = jnp.stack([col_sums[0], col_sums[2]])
    first_grad = lax.psum_scatter(
        jnp.einsum("rjc,djc->rd", qkv_grad, qkv_weight, preferred_element_type=jnp.float32),
        "mp",
        scatter_dimension=0,
        tiled=True,
    )
    first_gain_grad = jnp.sum(first_grad * first_hat, axis=0)
    first_shift_grad = jnp.sum(first_grad, axis=0)
    input_grad = mid_grad + norm_back(first_grad * first_gain, first_hat, first_inv)
    seq_part = lax.dot_general(select, input_grad, (((0,), (0,)), ((), ())), precision=HIGHEST)
    (
        qkv_weight_grad,
        qv_bias_grad,
        out_weight_grad,
        in_weight_grad,
        in_bias_grad,
        back_weight_grad,
    ) = lax.psum(
        (
            qkv_weight_grad,
            qv_bias_grad,
            out_weight_grad,
            in_weight_grad,
            in_bias_grad,
            back_weight_grad,
        ),
        "dp",
    )
    table_part = jax.ops.segment_sum(seq_part, timesteps, num_segments=NSTEPS)
    (
        first_gain_grad,
        first_shift_grad,
        second_gain_grad,
        second_shift_grad,
        out_bias_grad,
        back_bias_grad,
        table_grad,
    ) = lax.psum(
        (
            first_gain_grad,
            first_shift_grad,
            second_gain_grad,
            second_shift_grad,
            out_bias_grad,
            back_bias_grad,
            table_part,
        ),
        ("dp", "mp"),
    )
    return (
        output,
        input_grad,
        table_grad,
        qkv_weight_grad,
        qv_bias_grad,
        out_weight_grad,
        out_bias_grad,
        first_gain_grad,
        first_shift_grad,
        second_gain_grad,
        second_shift_grad,
        in_weight_grad,
        in_bias_grad,
        back_weight_grad,
        back_bias_grad,
    )


def solution(mesh):
    in_specs = (
        P(("dp", "mp"), None),
        P("dp"),
        P(("dp", "mp")),
        P(("dp", "mp"), None),
        P(),
        P(None, None, "mp"),
        P(None, "mp"),
        P("mp", None),
        P(),
        P(),
        P(),
        P(),
        P(),
        P(None, "mp"),
        P("mp"),
        P("mp", None),
        P(),
    )
    out_specs = (
        P(("dp", "mp"), None),
        P(("dp", "mp"), None),
        P(),
        P(None, None, "mp"),
        P(None, "mp"),
        P("mp", None),
        P(),
        P(),
        P(),
        P(),
        P(),
        P(None, "mp"),
        P("mp"),
        P("mp", None),
        P(),
    )
    return jax.shard_map(shards, mesh=mesh, in_specs=in_specs, out_specs=out_specs, check_vma=False)
```

profile of v0, /device:TPU:0, one launch (start us, length us, event | category | flops | bytes accessed | tf_op | source)
XLA Modules:
  0.0 1139.8 jit_solution(5077925286009492680)
XLA Ops:
  9.6 2.1 fusion.63
  14.3 66.1 %all-gather.5.cloned.1.call-done = bf16[2048,768]{1,0:T(8,128)(2,1)} async-done(((bf16[512,768]{1,0:T(8,128)(2,1)}), bf16[2048,768]{1,0:T(8,128)(2,1)}) %all-gather.5.cloned.1.call-update) | async-done | bytes 3145744 | tf_op jit(solution)/shard_map/all_gather | solution.py:149
  80.4 3.9 fusion.64
  84.4 1.7 add_convert_fusion
  86.1 6.6 reshape.190
  92.7 3.8 copy.51
  96.5 22.4 %while.50 = (s32[]{:T(128)}, bf16[2,1024,192]{1,2,0:T(8,128)(2,1)S(1)}, f32[2,2,3,512]{3,2,1,0:T(4,128)S(1)}, bf16[2,1024,3,3,64]{1,4,3,2,0:T(8,128)(2,1)}, s32[]{:T(128)}, /*index=5*/s32[]{:T(128)}, s32[]{:T(128)}) while((s32[]{:T(128)}, bf16[2,1024,192]{1,2,0:T(8,128)(2,1)S(1)}, f32[2,2,3,512]{3,2,1,0:T(4,128)S(1)}, ...), condition=%wide.region_7.8_spmd, body=%wide.region_2.7_spmd.sunk | while | flops 416905728 | bytes 28797184 | solution.py:156
  96.5 1.4 dynamic-slice_bitcast_fusion.8
  98.4 8.6 while.53
  100.8 1.8 fusion.140
  105.1 1.8 fusion.140
  109.6 8.6 while.53
  112.0 1.8 fusion.140
  116.3 1.8 fusion.140
  119.0 3.7 fusion.65
  123.3 109.0 %reduce-scatter.5.cloned.1.call-done = f32[512,768]{1,0:T(8,128)} async-done(((f32[2048,768]{1,0:T(8,128)}), f32[512,768]{1,0:T(8,128)}) %reduce-scatter.5.cloned.1.call-update) | async-done | bytes 1572880 | tf_op jit(solution)/shard_map/reduce_scatter | solution.py:158
  232.3 1.7 fusion.60
  236.4 1.7 convert_reduce_fusion.2
  238.3 62.3 %all-gather.7.cloned.1.call-done = bf16[2048,768]{1,0:T(8,128)(2,1)} async-done(((bf16[512,768]{1,0:T(8,128)(2,1)}), bf16[2048,768]{1,0:T(8,128)(2,1)}) %all-gather.7.cloned.1.call-update) | async-done | bytes 3145744 | tf_op jit(solution)/shard_map/all_gather | solution.py:171
  300.5 7.2 fusion.66
  307.7 57.0 %all-gather.9.cloned.1.call-done = bf16[2048,768]{1,0:T(8,128)(2,1)} async-done(((bf16[512,768]{1,0:T(8,128)(2,1)}), bf16[2048,768]{1,0:T(8,128)(2,1)}) %all-gather.9.cloned.1.call-update) | async-done | bytes 3145744 | tf_op jit(solution)/shard_map/all_gather | solution.py:182
  364.7 12.4 %convert_reduce_fusion = (f32[768]{0:T(1024)}, bf16[2048,768]{1,0:T(8,128)(2,1)S(1)}, bf16[2048,768]{1,0:T(8,128)(2,1)}) fusion(f32[2048,768]{1,0:T(8,128)} %fusion.66, f32[768]{0:T(1024)S(1)} %convert_element_type.81, bf16[2048,768]{1,0:T(8,128)(2,1)} %all-gather.9.cloned.1.call-done, bf16[768,768]{1,0:T(8,128)(2,1)S(1)} %copy-done.50), kind=kOutput, calls=%fused_computation.68 | convolution fusion | flops 2455239936 | bytes 16914432 | tf_op jit(solution)/shard_map/dot_general | solution.py:36
  377.1 1.7 copy-done.53
  378.8 4.6 fusion.68
  383.4 7.3 fusion.67
  391.0 101.9 %reduce-scatter.9.cloned.1.call-done = f32[512,768]{1,0:T(8,128)} async-done(((f32[2048,768]{1,0:T(8,128)}), f32[512,768]{1,0:T(8,128)}) %reduce-scatter.9.cloned.1.call-update) | async-done | bytes 1572880 | tf_op jit(solution)/shard_map/reduce_scatter | solution.py:188
  492.9 2.7 multiply_reduce_fusion.2
  495.7 110.7 %reduce-scatter.7.cloned.1.call-done = f32[512,768]{1,0:T(8,128)} async-done(((f32[2048,768]{1,0:T(8,128)}), f32[512,768]{1,0:T(8,128)}) %reduce-scatter.7.cloned.1.call-update) | async-done | bytes 1572880 | tf_op jit(solution)/shard_map/reduce_scatter | solution.py:176
  606.4 4.9 convert_reduce_fusion.3
  611.4 64.1 %all-gather.11.cloned.1.call-done = bf16[2048,768]{1,0:T(8,128)(2,1)} async-done(((bf16[512,768]{1,0:T(8,128)(2,1)}), bf16[2048,768]{1,0:T(8,128)(2,1)}) %all-gather.11.cloned.1.call-update) | async-done | bytes 3145744 | tf_op jit(solution)/shard_map/all_gather | solution.py:198
  675.5 3.0 convolution_convert_fusion
  679.4 51.3 %while.52 = (s32[]{:T(128)}, bf16[2,1024,3,3,64]{1,4,3,2,0:T(8,128)(2,1)}, bf16[2,1024,3,3,64]{1,4,3,2,0:T(8,128)(2,1)}, bf16[2,1024,3,64]{1,3,2,0:T(8,128)(2,1)...) while((s32[]{:T(128)}, ...), condition=%wide.region_19.20_spmd, body=%wide.region_15.19_spmd.sunk | while | flops 1030519296 | bytes 96016920 | solution.py:205
  683.8 16.3 %while.54 = (s32[]{:T(128)}, f32[1024,3,64]{0,2,1:T(8,128)S(1)}, f32[1024,3,64]{0,2,1:T(8,128)S(1)}, bf16[2,512,3,64]{1,3,2,0:T(8,128)(2,1)}, bf16[2,512,3,64]{1...) while((s32[]{:T(128)}, f32[1024,3,64]{0,2,1:T(8,128)S(1)}, ...), condition=%wide.region_18.18_spmd.clone, body=%wide.region_16.17_spmd.clone.sunk | while | flops 1026587136 | bytes 55883980 | solution.py:107
  684.9 1.4 fusion.135
  686.3 2.2 multiply_reduce_fusion.12
  688.5 1.6 multiply_convert_fusion.5
  693.0 1.4 fusion.135
  694.4 2.2 multiply_reduce_fusion.12
  696.6 1.6 multiply_convert_fusion.5
  701.9 1.5 copy-done.14
  709.4 16.3 %while.54 = (s32[]{:T(128)}, f32[1024,3,64]{0,2,1:T(8,128)S(1)}, f32[1024,3,64]{0,2,1:T(8,128)S(1)}, bf16[2,512,3,64]{1,3,2,0:T(8,128)(2,1)}, bf16[2,512,3,64]{1...) while((s32[]{:T(128)}, f32[1024,3,64]{0,2,1:T(8,128)S(1)}, ...), condition=%wide.region_18.18_spmd.clone, body=%wide.region_16.17_spmd.clone.sunk | while | flops 1026587136 | bytes 55883980 | solution.py:107
  710.5 1.4 fusion.135
  711.9 2.2 multiply_reduce_fusion.12
  714.1 1.6 multiply_convert_fusion.5
  720.1 2.2 multiply_reduce_fusion.12
  722.3 1.6 multiply_convert_fusion.5
  727.6 1.5 copy-done.14
  730.6 5.5 copy.55
  736.1 6.8 reshape.193
  743.0 7.0 convolution_bitcast_fusion
  750.1 7.1 fusion.71
  757.1 4.1 fusion.70
  763.4 1.6 fusion.69
  765.5 3.2 fusion.72
  769.0 90.5 %reduce-scatter.11.cloned.1.call-done = f32[512,768]{1,0:T(8,128)} async-done(((f32[2048,768]{1,0:T(8,128)}), f32[512,768]{1,0:T(8,128)}) %reduce-scatter.11.cloned.1.call-update) | async-done | bytes 1572880 | tf_op jit(solution)/shard_map/reduce_scatter | solution.py:213
  859.6 2.3 multiply_reduce_fusion.3
  861.9 1.9 multiply_add_fusion
  865.7 2.5 scatter_custom_fusion
  868.3 2.2 convert_reduce_fusion.1
  870.7 15.4 %all-reduce.1 = (f32[2,192]{1,0:T(2,128)}, f32[768]{0:T(1024)}) all-reduce(f32[2,192]{1,0:T(2,128)S(1)} %pad_maximum_fusion.1, f32[768]{0:T(1024)S(1)} %copy-done.43), channel_id=1, replica_groups=mesh['dp'=8,'mp'=4] {'dp'}, use_global_device_ids=true, to_apply=%region_27.28 | all-reduce | flops 1152 | bytes 9216 | tf_op jit(solution)/shard_map/psum | solution.py:230
  886.1 41.2 %all-reduce = (f32[768]{0:T(1024)}, f32[768]{0:T(1024)}, f32[768]{0:T(1024)}, f32[768]{0:T(1024)}, f32[768]{0:T(1024)}, /*index=5*/f32[768]{0:T(1024)}) all-reduce(f32[768]{0:T(1024)S(1)} %copy-done.38, f32[768]{0:T(1024)S(1)} %get-tuple-element.239, f32[768]{0:T(1024)S(1)} %get-tuple-element.244, ...), channel_id=1, replica_groups=mesh['dp'=8,'mp'=4] {'dp','mp'}, use_global_device_ids=true, to_apply=%region_30.31 | all-reduce | flops 4608 | bytes 36864 | tf_op jit(solution)/shard_map/psum | solution.py:250
  927.4 51.7 %all-reduce.8.cloned.1.call-done = (f32[768,3,192]{0,2,1:T(8,128)}, f32[192,768]{1,0:T(8,128)}, f32[768,768]{1,0:T(8,128)}, f32[768,768]{1,0:T(8,128)}) async-done(((f32[768,3,192]{0,2,1:T(8,128)}, f32[192,768]{1,0:T(8,128)}, f32[768,768]{1,0:T(8,128)}, f32[768,768]{1,0:T(8,128)}), (f32[768,3,192]{0,2,1:T(8,128)}, f32[192,768]{1,0:T(8,128)}, f32[768,768]{1,0:T(8,128)}, ...) | async-done | bytes 7077904 | tf_op jit(solution)/shard_map/psum | solution.py:230
  979.1 143.0 %all-reduce.6.cloned.1.call-done = f32[1000,768]{1,0:T(8,128)} async-done(((f32[1000,768]{1,0:T(8,128)}), f32[1000,768]{1,0:T(8,128)}) %all-reduce.6.cloned.1.call-update) | async-done | bytes 3072016 | tf_op jit(solution)/shard_map/psum | solution.py:250
  1122.1 3.8 copy.119
  (259 shorter events, 62.6 us)
Async XLA Ops:
  7.2 73.2 %all-gather.5.cloned.1.call-start = ((), (), s32[]{:S(2)}) async-start(), calls=%async_computation.4 | async-start | bytes 3932160 | tf_op jit(solution)/shard_map/all_gather | solution.py:149
  8.6 3.1 copy-start.33
  9.6 3.3 copy-start.29
  9.6 3.3 copy-start.39
  11.7 2.3 copy-start.26
  11.7 2.5 copy-start.45
  11.8 68.7 %copy-start.51 = (bf16[768,3,192]{0,2,1:T(8,128)(2,1)S(1)}, bf16[768,3,192]{0,2,1:T(8,128)(2,1)}, u32[]{:S(2)}) copy-start(bf16[768,3,192]{0,2,1:T(8,128)(2,1)} %param.30) | copy-start | bytes 2654212
  12.9 71.5 %copy-start.31 = (f32[512]{0:T(512)}, f32[512]{0:T(512)S(1)}, u32[]{:S(2)}) copy-start(f32[512]{0:T(512)S(1)} %add_rsqrt_fusion.1) | copy-start | bytes 6148
  14.1 218.2 %reduce-scatter.5.cloned.1.call-start = ((), (), s32[]{:S(2)}) async-start(), calls=%async_computation.5 | async-start | bytes 7864320 | tf_op jit(solution)/shard_map/reduce_scatter | solution.py:158
  96.5 22.5 %copy-start.25 = (bf16[192,768]{1,0:T(8,128)(2,1)S(1)}, bf16[192,768]{1,0:T(8,128)(2,1)}, u32[]{:S(2)}) copy-start(bf16[192,768]{1,0:T(8,128)(2,1)} %param.32) | copy-start | bytes 884740
  119.0 3.7 copy-start.12
  122.7 109.6 %copy-start.3 = (f32[512,768]{1,0:T(8,128)S(1)}, f32[512,768]{1,0:T(8,128)}, u32[]{:S(2)}) copy-start(f32[512,768]{1,0:T(8,128)} %copy-done.2) | copy-start | bytes 4718596
  122.7 109.6 %copy-start.40 = (f32[768]{0:T(1024)S(1)}, f32[768]{0:T(1024)}, u32[]{:S(2)}) copy-start(f32[768]{0:T(1024)} %param.33) | copy-start | bytes 9220
  122.7 112.4 %copy-start.28 = (f32[768]{0:T(1024)S(1)}, f32[768]{0:T(1024)}, u32[]{:S(2)}) copy-start(f32[768]{0:T(1024)} %param.36) | copy-start | bytes 9220
  122.7 112.4 %copy-start.41 = (f32[768]{0:T(1024)S(1)}, f32[768]{0:T(1024)}, u32[]{:S(2)}) copy-start(f32[768]{0:T(1024)} %param.37) | copy-start | bytes 9220
  122.7 177.8 %all-gather.7.cloned.1.call-start = ((), (), s32[]{:S(2)}) async-start(), calls=%async_computation.6 | async-start | bytes 3932160 | tf_op jit(solution)/shard_map/all_gather | solution.py:171
  234.0 2.4 copy-start.46
  234.0 2.4 copy-start.23
  235.1 3.1 copy-start.44
  235.1 65.4 %copy-start.49 = (bf16[768,768]{1,0:T(8,128)(2,1)S(1)}, bf16[768,768]{1,0:T(8,128)(2,1)}, u32[]{:S(2)}) copy-start(bf16[768,768]{1,0:T(8,128)(2,1)} %param.38) | copy-start | bytes 3538948
  236.4 128.4 %all-gather.9.cloned.1.call-start = ((), (), s32[]{:S(2)}) async-start(), calls=%async_computation.8 | async-start | bytes 3932160 | tf_op jit(solution)/shard_map/all_gather | solution.py:182
  238.2 254.8 %reduce-scatter.9.cloned.1.call-start = ((), (), s32[]{:S(2)}) async-start(), calls=%async_computation.9 | async-start | bytes 7864320 | tf_op jit(solution)/shard_map/reduce_scatter | solution.py:188
  238.2 126.5 %copy-start.50 = (bf16[768,768]{1,0:T(8,128)(2,1)S(1)}, bf16[768,768]{1,0:T(8,128)(2,1)}, u32[]{:S(2)}) copy-start(bf16[768,768]{1,0:T(8,128)(2,1)} %param.40) | copy-start | bytes 3538948
  377.1 1.7 copy-start.53
  383.4 223.0 %reduce-scatter.7.cloned.1.call-start = ((), (), s32[]{:S(2)}) async-start(), calls=%async_computation.7 | async-start | bytes 7864320 | tf_op jit(solution)/shard_map/reduce_scatter | solution.py:176
  390.7 102.2 %copy-start.6 = (f32[512,768]{1,0:T(8,128)S(1)}, f32[512,768]{1,0:T(8,128)}, u32[]{:S(2)}) copy-start(f32[512,768]{1,0:T(8,128)} %copy-done.5) | copy-start | bytes 4718596
  390.8 215.6 %copy-start.16 = (bf16[512,768]{1,0:T(8,128)(2,1)S(1)}, bf16[512,768]{1,0:T(8,128)(2,1)}, u32[]{:S(2)}) copy-start(bf16[512,768]{1,0:T(8,128)(2,1)} %get-tuple-element.306) | copy-start | bytes 2359300
  390.8 215.6 %copy-start.42 = (f32[768]{0:T(1024)S(1)}, f32[768]{0:T(1024)}, u32[]{:S(2)}) copy-start(f32[768]{0:T(1024)} %param.41) | copy-start | bytes 9220
  390.8 284.7 %all-gather.11.cloned.1.call-start = ((), (), s32[]{:S(2)}) async-start(), calls=%async_computation.10 | async-start | bytes 3932160 | tf_op jit(solution)/shard_map/all_gather | solution.py:198
  611.3 248.2 %reduce-scatter.11.cloned.1.call-start = ((), (), s32[]{:S(2)}) async-start(), calls=%async_computation.11 | async-start | bytes 7864320 | tf_op jit(solution)/shard_map/reduce_scatter | solution.py:213
  688.5 1.6 copy-start.8
  696.6 1.6 copy-start.8
  701.8 1.7 copy-start.14
  701.9 3.1 copy-start.11
  703.6 1.4 copy-start.15
  714.1 1.6 copy-start.8
  722.2 1.6 copy-start.8
  727.4 1.7 copy-start.14
  727.6 3.1 copy-start.11
  729.2 1.4 copy-start.15
  736.1 6.8 copy-start.52
  750.0 229.1 %all-reduce.8.cloned.1.call-start = ((), (), s32[]{:S(2)}) async-start(), calls=%async_computation.13 | async-start | bytes 14155776 | tf_op jit(solution)/shard_map/psum | solution.py:230
  750.0 7.1 copy-start.48
  750.1 7.1 copy-start.54
  757.1 4.1 copy-start.7
  761.2 2.1 copy-start.19
  763.4 2.1 copy-start.47
  768.7 90.8 %copy-start.4 = (f32[512,768]{1,0:T(8,128)S(1)}, f32[512,768]{1,0:T(8,128)}, u32[]{:S(2)}) copy-start(f32[512,768]{1,0:T(8,128)} %copy-done.2) | copy-start | bytes 4718596
  768.7 90.8 %copy-start.27 = (f32[512]{0:T(512)S(1)}, f32[512]{0:T(512)}, u32[]{:S(2)}) copy-start(f32[512]{0:T(512)} %copy-done.26) | copy-start | bytes 6148
  768.7 90.8 %copy-start.30 = (f32[768]{0:T(1024)S(1)}, f32[768]{0:T(1024)}, u32[]{:S(2)}) copy-start(f32[768]{0:T(1024)} %param.34) | copy-start | bytes 9220
  768.7 90.8 %copy-start.32 = (f32[512]{0:T(512)S(1)}, f32[512]{0:T(512)}, u32[]{:S(2)}) copy-start(f32[512]{0:T(512)} %copy-done.31) | copy-start | bytes 6148
  768.7 353.4 %all-reduce.6.cloned.1.call-start = ((), (), s32[]{:S(2)}) async-start(), calls=%async_computation.12 | async-start | bytes 6144000 | tf_op jit(solution)/shard_map/psum | solution.py:250
  859.6 2.3 copy-start.18
  861.9 3.1 copy-start.34
  868.2 2.5 copy-start.43
  868.2 17.9 %copy-start.35 = (f32[768]{0:T(1024)S(1)}, f32[768]{0:T(1024)}, u32[]{:S(2)}) copy-start(f32[768]{0:T(1024)} %get-tuple-element.305) | copy-start | bytes 9220
  868.2 17.9 %copy-start.36 = (f32[768]{0:T(1024)S(1)}, f32[768]{0:T(1024)}, u32[]{:S(2)}) copy-start(f32[768]{0:T(1024)} %get-tuple-element.237) | copy-start | bytes 9220
  868.2 17.9 %copy-start.37 = (f32[768]{0:T(1024)S(1)}, f32[768]{0:T(1024)}, u32[]{:S(2)}) copy-start(f32[768]{0:T(1024)} %get-tuple-element.243) | copy-start | bytes 9220
  868.2 17.9 %copy-start.38 = (f32[768]{0:T(1024)S(1)}, f32[768]{0:T(1024)}, u32[]{:S(2)}) copy-start(f32[768]{0:T(1024)} %get-tuple-element.307) | copy-start | bytes 9220
  1122.1 3.8 copy-start.22
  1125.9 1.4 copy-start.24
  1125.9 2.7 copy-start.21
  1128.6 2.5 copy-start.20
  1128.6 3.9 copy-start.1
  (11 other events, 10.8 us)
Sparse Core Ops, SparseCore 0:
  14.2 66.1 all-gather.4
  122.8 109.3 reduce-scatter.4
  236.5 64.0 all-gather.6
  302.5 62.1 all-gather.8
  383.5 109.3 reduce-scatter.8
  495.1 111.2 reduce-scatter.6
  611.5 64.0 all-gather.10
  750.1 109.3 reduce-scatter.10
  863.8 115.2 all-reduce.7
  985.0 137.0 all-reduce.5
where the time goes:
time: 1150 us; the launch traced here: 1140 us
  waiting for transfers between devices  857 us (75%)
  matrix products  106 us (9%)
  local copies, waits for them, and re-layouts  65.9 us (6%)
  blocking collectives  56.6 us (5%)
  other arithmetic  37 us (3%)
  between operations  15.1 us (1%)
    psum x1, waiting for transfers between devices, shards(): lax.psum((first_gain_grad, first_shift_grad, second_gain_grad, second_shi...  143 us
    reduce_scatter x1, waiting for transfers between devices, shards(): lax.psum_scatter(jnp.dot(active, back_weight, preferred_element_type=jnp....  111 us
    reduce_scatter x1, waiting for transfers between devices, shards(): lax.psum_scatter(jnp.dot(attended, out_weight, preferred_element_type=jnp...  109 us
    reduce_scatter x1, waiting for transfers between devices, shards(): lax.psum_scatter(contract_cols(pre_grad, in_weight), 'mp', scatter_dimens...  102 us
    reduce_scatter x1, waiting for transfers between devices, shards(): lax.psum_scatter(jnp.einsum('rjc,djc->rd', qkv_grad, qkv_weight, preferre...  90.5 us
    all_gather x1, waiting for transfers between devices, shards(): first_all = lax.all_gather(normed_one, 'mp', axis=0, tiled=True)  66.1 us
    all_gather x1, waiting for transfers between devices, shards(): branch_all = lax.all_gather(branch_low, 'mp', axis=0, tiled=True)  64.1 us
    all_gather x1, waiting for transfers between devices, shards(): second_all = lax.all_gather(normed_two, 'mp', axis=0, tiled=True)  62.3 us
  transfers between devices with their start and end apart: 10, of which 10 were waited for; matrix products, arithmetic and copies ran while one was open for 4% of the time, Pallas kernels for 0%

commit v1 on v0

v1 whole, which is shorter than its diff:
```python
import functools

import jax
import jax.numpy as jnp
from jax import lax
from jax.experimental import pallas as pl
from jax.experimental.pallas import tpu as pltpu
from jax.sharding import Mesh, PartitionSpec as P

HEAD_DIM = 64
NSTEPS = 1000
L = 1024
EPSILON = 1e-05
HIGHEST = lax.Precision.HIGHEST
MESH = pl.DeviceIdType.MESH
BF = jnp.bfloat16
F32 = jnp.float32


def place():
    k = lax.axis_index("k")
    c = lax.axis_index("c")
    z = lax.axis_index("mp")
    return k, c, z


def flip(i, bit):
    if bit == 1:
        return i + 1 - 2 * lax.rem(i, 2)
    if bit == 2:
        return lax.rem(i + 2, 4)
    return 3 - i


def enter_barrier():
    k, c, z = place()
    sem = pltpu.get_barrier_semaphore()
    peers = [{"c": 1 - c}, {"k": flip(k, 1)}, {"k": flip(k, 2)}] + [{"mp": flip(z, r)} for r in (1, 2, 3)]
    peers.append({"c": 1 - c, "mp": flip(z, 1)})
    for peer in peers:
        pl.semaphore_signal(sem, inc=1, device_id=peer, device_id_type=MESH)
    pl.semaphore_wait(sem, len(peers))


def remote(src, dst, ss, rs, peer):
    return pltpu.make_async_remote_copy(src_ref=src, dst_ref=dst, send_sem=ss, recv_sem=rs, device_id=peer, device_id_type=MESH)


def cut(ref, lead, q, k, half, c):
    first, count = {None: (0, q), 0: (0, (q // 32) * 16 if q % 32 else q // 2), 1: ((q // 32) * 16 if q % 32 else q // 2, 0)}[half]
    if half == 1:
        count = q - first
    start = pl.multiple_of(k * q + first, 16)
    cols = pl.ds(pl.multiple_of(c * 384, 128), 384)
    return ref.at[lead + (slice(None), pl.ds(start, count), cols)]


def cols_of(ref, lead, c):
    return ref.at[lead + (slice(None), slice(None), pl.ds(pl.multiple_of(c * 384, 128), 384))]


def gather_kernel(qkv_ref, out_ref, in_ref, back_ref, bias_ref, tok_ref, grad_ref, row_ref,
                  wa, wm, bias, tok, grad, row, local_sem, ssem, rsem, bsem, brem, wsem, wrem):
    k, c, z = place()
    kx, ky = flip(k, 1), flip(k, 2)
    nx, ny, nc = {"k": kx}, {"k": ky}, {"c": 1 - c}
    locals_ = [
        (qkv_ref, wa.at[0, pl.ds(0, 3)]),
        (out_ref, wa.at[0, 3]),
        (in_ref, wm.at[0, 0]),
        (back_ref, wm.at[0, 1]),
        (bias_ref, bias.at[0]),
    ]
    copies = [pltpu.make_async_copy(s, d, local_sem.at[i]) for i, (s, d) in enumerate(locals_)]
    for cp in copies:
        cp.start()
    enter_barrier()
    stays = c == lax.rem(z, 2)
    swap_peer = {"c": 1 - c, "mp": flip(z, 1)}
    swaps = [(tok_ref, tok), (row_ref, row), (grad_ref, grad)]
    remote_swaps = [remote(s, d, wsem.at[i], wrem.at[i], swap_peer) for i, (s, d) in enumerate(swaps)]
    local_swaps = [pltpu.make_async_copy(s, d, local_sem.at[5 + i]) for i, (s, d) in enumerate(swaps)]

    @pl.when(stays)
    def _():
        for cp in local_swaps:
            cp.start()

    @pl.when(jnp.logical_not(stays))
    def _():
        for cp in remote_swaps:
            cp.start()

    for cp in copies:
        cp.wait()
    small = [remote(bias.at[0], bias.at[r], bsem.at[r - 1], brem.at[r - 1], {"mp": flip(z, r)}) for r in (1, 2, 3)]
    for cp in small:
        cp.start()
    chunks = [(wa, 48, 1), (wa, 48, 2), (wa, 48, 3), (wm, 192, 1), (wm, 192, 2), (wm, 192, 3)]

    def sends(i):
        w, q, r = chunks[i]
        at = lambda ref, slot, kk, half: cut(ref, (slot,), q, kk, half, c)
        stage0 = [remote(at(w, 0, k, None), at(w, r, k, None), ssem.at[i, 0], rsem.at[i, 0], {"mp": flip(z, r)})]
        stage1 = [
            remote(at(w, r, k, None), at(w, r, k, None), ssem.at[i, 1], rsem.at[i, 1], nx),
            remote(at(w, r, k, None), at(w, r, k, None), ssem.at[i, 2], rsem.at[i, 2], ny),
        ]
        stage2 = [
            remote(at(w, r, ky, 0), at(w, r, ky, 0), ssem.at[i, 3], rsem.at[i, 3], nx),
            remote(at(w, r, kx, 1), at(w, r, kx, 1), ssem.at[i, 4], rsem.at[i, 4], ny),
        ]
        stage3 = [remote(cols_of(w, (r,), c), cols_of(w, (r,), c), ssem.at[i, 5], rsem.at[i, 5], nc)]
        return [stage0, stage1, stage2, stage3]

    def lands(i):
        w, q, r = chunks[i]
        at = lambda ref, slot, kk, half: cut(ref, (slot,), q, kk, half, c)
        kd = flip(k, 3)
        return [
            [(at(w, r, k, None), rsem.at[i, 0])],
            [(at(w, r, kx, None), rsem.at[i, 1]), (at(w, r, ky, None), rsem.at[i, 2])],
            [(at(w, r, kd, 0), rsem.at[i, 3]), (at(w, r, kd, 1), rsem.at[i, 4])],
            [(cols_of(w, (r,), 1 - c), rsem.at[i, 5])],
        ]

    n = len(chunks)
    all_sends = [sends(i) for i in range(n)]
    all_lands = [lands(i) for i in range(n)]
    for i in range(n):
        for cp in all_sends[i][0]:
            cp.start()
    for step in range(n + 3):
        for stage in range(4):
            i = step - stage
            if 0 <= i < n:
                for ref, sem in all_lands[i][stage]:
                    pltpu.make_async_copy(ref, ref, sem).wait()
                if stage < 3:
                    for cp in all_sends[i][stage + 1]:
                        cp.start()
    for i in range(n):
        for stage in all_sends[i]:
            for cp in stage:
                cp.wait_send()
    for cp in small:
        cp.wait()

    @pl.when(stays)
    def _():
        for cp in local_swaps:
            cp.wait()

    @pl.when(jnp.logical_not(stays))
    def _():
        for cp in remote_swaps:
            cp.wait()


def gather_weights(qkv, out, win, back, bias, tok, grad, row):
    hbm = pl.BlockSpec(memory_space=pl.ANY)
    shapes = (
        jax.ShapeDtypeStruct((4, 4, 192, 768), BF),
        jax.ShapeDtypeStruct((4, 2, 768, 768), BF),
        jax.ShapeDtypeStruct((4, 8, 768), F32),
        jax.ShapeDtypeStruct((512, 768), BF),
        jax.ShapeDtypeStruct((512, 768), BF),
        jax.ShapeDtypeStruct((16, 768), BF),
    )
    dma = pltpu.SemaphoreType.DMA
    return pl.pallas_call(
        gather_kernel,
        out_shape=shapes,
        in_specs=[hbm] * 8,
        out_specs=[hbm] * 6,
        scratch_shapes=[dma((8,)), dma((6, 6)), dma((6, 6)), dma((3,)), dma((3,)), dma((3,)), dma((3,))],
        compiler_params=pltpu.CompilerParams(collective_id=0, has_side_effects=True),
        name="gather_weights",
    )(qkv, out, win, back, bias, tok, grad, row)


def reduce_kernel(ga_ref, gm_ref, small_ref, seq_ref, og_ref, oo_ref,
                  outa, outm, small_out, seq_out, og_out, oo_out,
                  ga, gm, cra, crm, raa, rba, ram, rbm, bxa, bya, bxm, bym, za, zm, fa, fm, hyper,
                  local_sem, ssem, rsem, fsem, frem, hsem, hrem, qsem, qrem, wsem, wrem):
    k, c, z = place()
    kx, ky, kd = flip(k, 1), flip(k, 2), flip(k, 3)
    nx, ny, nc = {"k": kx}, {"k": ky}, {"c": 1 - c}
    copies = [pltpu.make_async_copy(ga_ref, ga, local_sem.at[0]), pltpu.make_async_copy(gm_ref, gm, local_sem.at[1]),
              pltpu.make_async_copy(small_ref, hyper.at[0], local_sem.at[2])]
    me = k * 8 + c * 4 + z
    copies.append(pltpu.make_async_copy(seq_ref, seq_out.at[me], local_sem.at[3]))
    for cp in copies:
        cp.start()
    enter_barrier()
    for cp in copies:
        cp.wait()
    stays = c == lax.rem(z, 2)
    swap_peer = {"c": 1 - c, "mp": flip(z, 1)}
    swaps = [(og_ref, og_out), (oo_ref, oo_out)]
    remote_swaps = [remote(s, d, wsem.at[i], wrem.at[i], swap_peer) for i, (s, d) in enumerate(swaps)]
    local_swaps = [pltpu.make_async_copy(s, d, local_sem.at[4 + i]) for i, (s, d) in enumerate(swaps)]

    @pl.when(stays)
    def _():
        for cp in local_swaps:
            cp.start()

    @pl.when(jnp.logical_not(stays))
    def _():
        for cp in remote_swaps:
            cp.start()

    chunks = [(gm, crm, r, 1, 192, ram, rbm, bxm, bym, zm) for r in range(4)]
    chunks += [(ga, cra, 2 * h, 2, 48, raa, rba, bxa, bya, za) for h in range(2)]
    mine = pl.ds(pl.multiple_of(c * 384, 128), 384)
    other = pl.ds(pl.multiple_of((1 - c) * 384, 128), 384)

    def part(q, half):
        first = (q // 32) * 16 if q % 32 else q // 2
        return (0, q) if half is None else ((0, first) if half == 0 else (first, q - first))

    def rows(q, kk, half):
        first, count = part(q, half)
        return pl.ds(pl.multiple_of(kk * q + first, 16), count)

    def make(i):
        g, cr, s0, ns, q, ra, rb, bx, by, zz = chunks[i]
        ss = pl.ds(s0, ns)
        every = slice(None)
        st = {}
        st["core"] = [remote(g.at[ss, every, every, other], cr.at[ss], ssem.at[i, 0], rsem.at[i, 0], nc)]
        st["a"] = [
            remote(g.at[ss, every, rows(q, kd, 0), mine], ra.at[ss], ssem.at[i, 1], rsem.at[i, 1], nx),
            remote(g.at[ss, every, rows(q, kd, 1), mine], rb.at[ss], ssem.at[i, 2], rsem.at[i, 2], ny),
        ]
        st["b"] = [
            remote(g.at[ss, every, rows(q, kx, None), mine], bx.at[ss], ssem.at[i, 3], rsem.at[i, 3], nx),
            remote(g.at[ss, every, rows(q, ky, None), mine], by.at[ss], ssem.at[i, 4], rsem.at[i, 4], ny),
        ]
        st["z"] = [
            remote(g.at[r, every, rows(q, k, None), mine], zz.at[r - 1], ssem.at[i, 4 + r], rsem.at[i, 4 + r], {"mp": flip(z, r)})
            for r in range(max(s0, 1), s0 + ns)
        ]
        return st

    all_sends = [make(i) for i in range(len(chunks))]

    def start(cps):
        for cp in cps:
            cp.start()

    def got(cps):
        for cp in cps:
            cp.wait_recv()

    def add_into(dst, pieces):
        n, m = dst.shape[0], dst.shape[1]
        for a in range(n):
            for b in range(m):
                total = dst[a, b].astype(F32)
                for p in pieces:
                    total = total + p[a, b].astype(F32)
                dst[a, b] = total.astype(BF)

    def core_add(i):
        g, cr, s0, ns, q, *_ = chunks[i]

        @pl.loop(0, 4)
        def _(j):
            r = pl.ds(pl.multiple_of(j * q, 16), q)
            add_into(g.at[pl.ds(s0, ns), :, r, mine], [cr.at[pl.ds(s0, ns), :, r]])

    def a_add(i):
        g, cr, s0, ns, q, ra, rb, *_ = chunks[i]
        ss = pl.ds(s0, ns)
        add_into(g.at[ss, :, rows(q, ky, 0), mine], [ra.at[ss]])
        add_into(g.at[ss, :, rows(q, kx, 1), mine], [rb.at[ss]])

    def b_add(i):
        g, cr, s0, ns, q, ra, rb, bx, by, zz = chunks[i]
        ss = pl.ds(s0, ns)
        add_into(g.at[ss, :, rows(q, k, None), mine], [bx.at[ss], by.at[ss]])

    steps = [
        (lambda i: None, "core"),
        (core_add, "a"),
        (a_add, "b"),
        (b_add, "z"),
    ]
    names = ["core", "a", "b", "z"]
    n = len(chunks)
    for step in range(n + 4):
        for stage in range(5):
            i = step - stage
            if 0 <= i < n:
                if stage > 0:
                    got(all_sends[i][names[stage - 1]])
                if stage < 4:
                    steps[stage][0](i)
                    start(all_sends[i][names[stage]])
    finals = [(gm, zm, fm, 192, 0), (ga, za, fa, 48, 1)]
    gathers = []
    for g, zz, f, q, j in finals:
        m = g.shape[1]
        for b in range(m):
            total = g[0, b, rows(q, k, None), mine].astype(F32)
            for r in range(3):
                total = total + zz[r, b].astype(F32)
            f[b, rows(q, k, None), mine] = total.astype(BF)
        at = lambda kk, half: f.at[:, rows(q, kk, half), mine]
        g1 = [remote(at(k, None), at(k, None), fsem.at[j, 0], frem.at[j, 0], nx),
              remote(at(k, None), at(k, None), fsem.at[j, 1], frem.at[j, 1], ny)]
        g2 = [remote(at(ky, 0), at(ky, 0), fsem.at[j, 2], frem.at[j, 2], nx),
              remote(at(kx, 1), at(kx, 1), fsem.at[j, 3], frem.at[j, 3], ny)]
        g3 = [remote(f.at[:, :, mine], f.at[:, :, mine], fsem.at[j, 4], frem.at[j, 4], nc)]
        start(g1)
        gathers.append((g1, g2, g3))
    peers = [nc, nx, ny, {"mp": flip(z, 1)}, {"mp": flip(z, 2)}]
    hops = []
    seqs = []
    spans = [
        lambda kk, cc, zz_: (pl.ds(kk * 8 + cc * 4 + zz_, 1),),
    ]
    for t, peer in enumerate(peers):
        cp = remote(hyper.at[2 * t], hyper.at[2 * t + 1], hsem.at[t], hrem.at[t], peer)
        cp.start()
        hops.append(cp)
        if t < 2:
            for g1, g2, g3 in gathers:
                got([g1, g2][t])
                start([g2, g3][t])
        cp.wait_recv()
        hyper[2 * t + 2] = hyper[2 * t] + hyper[2 * t + 1]
    done = pltpu.make_async_copy(hyper.at[10], small_out, local_sem.at[6])
    done.start()
    zs = [remote(seq_ref, seq_out.at[me], qsem.at[r - 1], qrem.at[r - 1], {"mp": flip(z, r)}) for r in (1, 2, 3)]
    start(zs)
    got(zs)
    line = lambda kk, cc: seq_out.at[pl.ds(kk * 8 + cc * 4, 4)]
    c1 = [remote(line(k, c), line(k, c), qsem.at[3], qrem.at[3], nc)]
    start(c1)
    got(c1)
    chip = lambda kk: seq_out.at[pl.ds(kk * 8, 8)]
    x1 = [remote(chip(k), chip(k), qsem.at[4], qrem.at[4], nx), remote(chip(k), chip(k), qsem.at[5], qrem.at[5], ny)]
    start(x1)
    got(x1)
    x2 = [remote(chip(ky), chip(ky), qsem.at[6], qrem.at[6], nx)]
    start(x2)
    got(x2)
    for g1, g2, g3 in gathers:
        got(g3)
    outs = [pltpu.make_async_copy(fa, outa, local_sem.at[7]), pltpu.make_async_copy(fm, outm, local_sem.at[8])]
    start(outs)
    for cp in zs + c1 + x1 + x2 + hops:
        cp.wait_send()
    for g in gathers:
        for stage in g:
            for cp in stage:
                cp.wait_send()
    for st in all_sends:
        for stage in st.values():
            for cp in stage:
                cp.wait_send()
    for cp in outs + [done]:
        cp.wait()

    @pl.when(stays)
    def _():
        for cp in local_swaps:
            cp.wait()

    @pl.when(jnp.logical_not(stays))
    def _():
        for cp in remote_swaps:
            cp.wait()


def reduce_grads(ga, gm, small, seq, og, oo):
    hbm = pl.BlockSpec(memory_space=pl.ANY)
    dma = pltpu.SemaphoreType.DMA
    vm = pltpu.VMEM
    shapes = (
        jax.ShapeDtypeStruct((4, 192, 768), BF),
        jax.ShapeDtypeStruct((2, 768, 768), BF),
        jax.ShapeDtypeStruct(small.shape, F32),
        jax.ShapeDtypeStruct((32,) + seq.shape, F32),
        jax.ShapeDtypeStruct(og.shape, F32),
        jax.ShapeDtypeStruct(oo.shape, BF),
    )
    scratch = [
        vm((4, 4, 192, 768), BF),
        vm((4, 2, 768, 768), BF),
        vm((4, 4, 192, 384), BF),
        vm((4, 2, 768, 384), BF),
        vm((4, 4, 16, 384), BF),
        vm((4, 4, 32, 384), BF),
        vm((4, 2, 96, 384), BF),
        vm((4, 2, 96, 384), BF),
        vm((4, 4, 48, 384), BF),
        vm((4, 4, 48, 384), BF),
        vm((4, 2, 192, 384), BF),
        vm((4, 2, 192, 384), BF),
        vm((3, 4, 48, 384), BF),
        vm((3, 2, 192, 384), BF),
        vm((4, 192, 768), BF),
        vm((2, 768, 768), BF),
        vm((11,) + small.shape, F32),
        dma((9,)), dma((6, 8)), dma((6, 8)), dma((2, 5)), dma((2, 5)), dma((5,)), dma((5,)), dma((7,)), dma((7,)), dma((2,)), dma((2,)),
    ]
    return pl.pallas_call(
        reduce_kernel,
        out_shape=shapes,
        in_specs=[hbm] * 6,
        out_specs=[hbm] * 6,
        scratch_shapes=scratch,
        compiler_params=pltpu.CompilerParams(collective_id=1, has_side_effects=True, vmem_limit_bytes=60 << 20),
        name="reduce_grads",
    )(ga, gm, small, seq, og, oo)


def norm_parts(values):
    center = values - jnp.mean(values, axis=-1, keepdims=True)
    inverse = lax.rsqrt(jnp.mean(center * center, axis=-1, keepdims=True) + EPSILON)
    return (center * inverse, inverse)


def norm_back(upstream, normal, inverse):
    return inverse * (
        upstream
        - jnp.mean(upstream, axis=-1, keepdims=True)
        - normal * jnp.mean(upstream * normal, axis=-1, keepdims=True)
    )


def dots(spec, a, b):
    return jnp.einsum(spec, a, b, preferred_element_type=F32)


def shards(tokens, timesteps, masked, cotangent, step_table, qkv_weight, qv_bias, out_weight, out_bias,
           first_gain, first_shift, second_gain, second_shift, in_weight, in_bias, back_weight, back_bias):
    z = lax.axis_index("mp")
    c = lax.axis_index("c")
    seq = z // 2
    step = lax.dynamic_index_in_dim(timesteps, seq, keepdims=False)
    row = lax.dynamic_slice_in_dim(step_table, step, 1, axis=0)
    row16 = jnp.broadcast_to(row, (16, 768))
    grad_low = cotangent * masked.astype(BF)[:, None]
    bias = jnp.zeros((8, 768), F32).at[0].set(in_bias.astype(F32)).at[1, :192].set(qv_bias[0]).at[2, :192].set(qv_bias[1])
    wa, wm, biases, tok, grad, row_in = gather_weights(
        qkv_weight.transpose(1, 2, 0), out_weight, in_weight, back_weight, bias, tokens, grad_low, row16)
    stream = tok.astype(F32) + row_in[:1].astype(F32)
    first_hat, first_inv = norm_parts(stream)
    normed_one = (first_hat * first_gain + first_shift).astype(BF)
    qkv_bias = jnp.stack([biases[:, 1, :192], jnp.zeros((4, 192), F32), biases[:, 2, :192]], axis=1)
    proj = (dots("rd,spcd->rspc", normed_one, wa[:, :3]) + qkv_bias).astype(BF)
    heads = proj.reshape(512, 4, 3, 3, 64)
    q = heads[:, :, 0].reshape(512, 12, 64)
    kv = lax.all_gather(heads[:, :, 1:], "c", axis=0, tiled=True)
    keys = kv[:, :, 0].reshape(1024, 12, 64)
    vals = kv[:, :, 1].reshape(1024, 12, 64)
    scale = HEAD_DIM ** (-0.5)
    s = dots("qhc,khc->hqk", q, keys) * scale
    probs = jax.nn.softmax(s, axis=-1)
    low_probs = probs.astype(BF)
    attended = dots("hqk,khc->qhc", low_probs, vals).astype(BF).reshape(512, 768)
    wo = wa[:, 3].reshape(768, 768)
    branch = dots("rc,cd->rd", attended, wo)
    mid = stream + (branch + out_bias)
    second_hat, second_inv = norm_parts(mid)
    normed_two = (second_hat * second_gain + second_shift).astype(BF)
    grad_out = grad.astype(F32)
    preact = dots("rd,sdh->srh", normed_two, wm[:, 0]) + biases[:, 0][:, None, :]
    active = jax.nn.gelu(preact).astype(BF)
    feed = dots("srh,shd->rd", active, wm[:, 1])
    output = (mid + (feed + back_bias)).astype(BF)
    back_g = dots("srh,rd->shd", active, grad).astype(BF)
    pullback = jax.vjp(jax.nn.gelu, preact)[1]
    pre_grad = pullback(dots("rd,shd->srh", grad, wm[:, 1]))[0].astype(BF)
    in_bias_g = jnp.sum(pre_grad.astype(F32), axis=1)
    in_g = dots("rd,srh->sdh", normed_two, pre_grad).astype(BF)
    second_grad = dots("srh,sdh->rd", pre_grad, wm[:, 0])
    back_bias_g = jnp.sum(grad_out, axis=0)
    second_gain_g = jnp.sum(second_grad * second_hat, axis=0)
    second_shift_g = jnp.sum(second_grad, axis=0)
    mid_grad = grad_out + norm_back(second_grad * second_gain, second_hat, second_inv)
    branch_low = mid_grad.astype(BF)
    out_bias_g = jnp.sum(branch_low.astype(F32), axis=0)
    out_g = dots("rc,rd->cd", attended, branch_low).astype(BF).reshape(4, 192, 768)
    att_grad = dots("rd,cd->rc", branch_low, wo).astype(BF).reshape(512, 12, 64)
    dval = dots("hqk,qhc->khc", low_probs, att_grad)
    dprob = dots("qhc,khc->hqk", att_grad, vals)
    ds = (probs * (dprob - jnp.sum(dprob * probs, axis=-1, keepdims=True))).astype(BF)
    dq = (dots("hqk,khc->qhc", ds, keys) * scale).astype(BF)
    dk = dots("hqk,qhc->khc", ds, q) * scale
    dkv = lax.psum_scatter(jnp.stack([dk, dval], axis=1), "c", scatter_dimension=0, tiled=True).astype(BF)
    qkv_g = jnp.stack([dq, dkv[:, 0], dkv[:, 1]], axis=1).reshape(512, 3, 4, 192)
    wqkv_g = dots("rpsc,rd->spcd", qkv_g, normed_one).astype(BF)
    ga = jnp.concatenate([wqkv_g, out_g[:, None]], axis=1)
    gm = jnp.stack([in_g, back_g], axis=1)
    col = jnp.sum(qkv_g.astype(F32), axis=0)
    first_grad = dots("rpsc,spcd->rd", qkv_g, wa[:, :3])
    first_gain_g = jnp.sum(first_grad * first_hat, axis=0)
    first_shift_g = jnp.sum(first_grad, axis=0)
    input_grad = mid_grad + norm_back(first_grad * first_gain, first_hat, first_inv)
    order = z ^ jnp.arange(4)
    pad = lambda v: jnp.pad(v, ((0, 0), (0, 576)))
    small = jnp.concatenate([
        jnp.take(in_bias_g, order, axis=0), jnp.take(pad(col[0]), order, axis=0), jnp.take(pad(col[2]), order, axis=0),
        first_gain_g[None], first_shift_g[None], second_gain_g[None], second_shift_g[None], out_bias_g[None], back_bias_g[None],
        jnp.zeros((6, 768), F32)])
    stays = c == z % 2
    seq_sum = jnp.zeros((8, 768), F32).at[0].set(jnp.sum(input_grad, axis=0))
    my_step = lax.all_gather(step.astype(F32), ("c", "mp"))
    src = jnp.where(stays, c * 4 + z, (1 - c) * 4 + (z ^ 1))
    seq_sum = seq_sum.at[1].set(my_step[src])
    outa, outm, small, seqs, input_grad, output = reduce_grads(ga, gm, small, seq_sum, input_grad, output)
    n_dh = lax.axis_size("dh")
    onehot = (jnp.arange(NSTEPS, dtype=jnp.int32)[:, None] == seqs[:, 1, 0].astype(jnp.int32)[None, :]).astype(F32)
    table = jnp.dot(onehot, seqs[:, 0], precision=HIGHEST)
    qkv_g = outa[:3].astype(F32)
    out_g = outa[3].astype(F32)
    in_g = outm[0].astype(F32)
    back_g = outm[1].astype(F32)
    if n_dh > 1:
        table, qkv_g, out_g, in_g, back_g, small = lax.psum((table, qkv_g, out_g, in_g, back_g, small), "dh")
    own = lambda first, n: lax.dynamic_index_in_dim(small[first:first + 4], z, keepdims=False)[:n]
    return (output, input_grad, table, qkv_g.transpose(2, 0, 1), jnp.stack([own(4, 192), own(8, 192)]), out_g, small[16],
            small[12], small[13], small[14], small[15], in_g, own(0, 768), back_g, small[17])


def solution(mesh):
    n_dp, n_mp = mesh.devices.shape
    fine = Mesh(mesh.devices.reshape(n_dp // 8, 4, 2, n_mp), ("dh", "k", "c", "mp"))
    dp = ("dh", "k", "c")
    rows = dp + ("mp",)
    in_specs = (P(rows, None), P(dp), P(rows), P(rows, None), P(), P(None, None, "mp"), P(None, "mp"), P("mp", None),
                P(), P(), P(), P(), P(), P(None, "mp"), P("mp"), P("mp", None), P())
    out_specs = (P(rows, None), P(rows, None), P(), P(None, None, "mp"), P(None, "mp"), P("mp", None), P(), P(), P(), P(), P(),
                 P(None, "mp"), P("mp"), P("mp", None), P())
    return jax.shard_map(shards, mesh=fine, in_specs=in_specs, out_specs=out_specs, check_vma=False)
```

time: 1150 us -> 564 us (0.49)
  waiting for transfers between devices: 857 us -> 5.44 us
  Pallas kernels: 0 us -> 306 us
  blocking collectives: 56.6 us -> 17.1 us
  local copies, waits for them, and re-layouts: 65.9 us -> 34.8 us
  other arithmetic: 37 us -> 55.5 us
  matrix products: 106 us -> 121 us
    reduce_scatter x4 -> x1, waiting for transfers between devices: 412 us -> 0.01 us  [shards(): lax.psum_scatter(jnp.stack([dk, dval], axis=1), 'c', scatter_dimension=0,...]
    pallas_call x0 -> x2, Pallas kernels: none -> 306 us  [the longest x1 177 us: gather_weights(): pl.pallas_call(gather_kernel, out_shape=shapes, in_specs=[hbm] * 8, out_s...]
    all_gather x4 -> x1, waiting for transfers between devices: 250 us -> 5.39 us  [shards(): kv = lax.all_gather(heads[:, :, 1:], 'c', axis=0, tiled=True)]
    psum x2 -> x0, waiting for transfers between devices: 195 us -> none  [the longest x1 143 us: shards(): lax.psum((first_gain_grad, first_shift_grad, second_gain_grad, second_shi...]
    psum x2 -> x0, blocking collectives: 56.6 us -> none  [the longest x1 41.2 us: shards(): lax.psum((first_gain_grad, first_shift_grad, second_gain_grad, second_shi...]
    while x43 -> x0, local copies, waits for them, and re-layouts: 19.4 us -> none
    unnamed x0 -> x1, blocking collectives: none -> 17.1 us
    reduce_sum x9 -> x3, other arithmetic: 19.1 us -> 3 us  [the longest x1 1.77 us: shards(): seq_sum = jnp.zeros((8, 768), F32).at[0].set(jnp.sum(input_grad, axis=0))]
  transfers between devices with their start and end apart: 10 -> 2, of which waited for: 10 -> 1; matrix products, arithmetic and copies ran while one was open for 4% -> 9% of each run, Pallas kernels for 0% -> 0%
where the time goes in v1:
time: 564 us; the launch traced here: 558 us
  Pallas kernels  306 us (54%)
  matrix products  121 us (21%)
  other arithmetic  55.5 us (10%)
  local copies, waits for them, and re-layouts  34.8 us (6%)
  between operations  17.9 us (3%)
  blocking collectives  17.1 us (3%)
    pallas_call x1, Pallas kernels, gather_weights(): pl.pallas_call(gather_kernel, out_shape=shapes, in_specs=[hbm] * 8, out_s...  177 us
    pallas_call x1, Pallas kernels, reduce_grads(): pl.pallas_call(reduce_kernel, out_shape=shapes, in_specs=[hbm] * 6, out_s...  130 us
    dot_general x16, matrix products, dots(): return jnp.einsum(spec, a, b, preferred_element_type=F32)  102 us
    unnamed x1, blocking collectives  17.1 us
    convert_element_type x1, other arithmetic, shards(): (probs * (dprob - jnp.sum(dprob * probs, axis=-1, keepdims=True))).astype...  16.3 us
    sub x1, matrix products, shards(): probs = jax.nn.softmax(s, axis=-1)  11.8 us
  transfers between devices with their start and end apart: 2, of which 1 were waited for; matrix products, arithmetic and copies ran while one was open for 9% of the time, Pallas kernels for 0%

profile of v1, /device:TPU:0, one launch (start us, length us, event | category | flops | bytes accessed | tf_op | source)
XLA Modules:
  0.0 558.5 jit_solution(16291157689509114598)
XLA Ops:
  7.3 1.3 dynamic_slice.20
  9.9 0.7 convert_element_type.119
  10.6 0.8 fusion.77
  11.4 0.7 reshape.242
  13.3 2.2 broadcast_multiply_fusion.grad_ref
  15.4 0.6 broadcast_in_dim.25.row_ref
  16.1 176.6 %gather_weights.1 = (bf16[4,4,192,768]{3,2,1,0:T(8,128)(2,1)}, bf16[4,2,768,768]{3,2,1,0:T(8,128)(2,1)}, f32[4,8,768]{2,1,0:T(8,128)}, bf16[512,768]{1,0:T(8,128...) custom-call(bf16[3,192,768]{2,1,0:T(8,128)(2,1)} %bitcast.195, bf16[192,768]{1,0:T(8,128)(2,1)} %out_ref.1, ...), custom_call_target="tpu_custom_call" | custom-call | tf_op jit(solution)/shard_map/gather_weights/pallas_call | solution.py:171
  192.7 0.7 convert_reduce_fusion.5
  193.4 1.4 fusion.47
  194.8 1.5 multiply_reduce_fusion.5
  196.3 0.8 fusion.75
  197.3 4.5 add_convert_fusion
  201.8 1.4 copy-done.14
  203.2 1.2 slice.227
  204.5 0.9 slice.201
  205.4 2.4 slice.198
  207.7 1.3 slice.229
  209.0 5.4 all-gather.2.cloned.1.call-done
  214.4 3.5 fusion.74
  217.9 11.8 %fusion.78 = (f32[12,512]{1,0:T(8,128)S(1)}, f32[12,512,1024]{2,1,0:T(8,128)}) fusion(bf16[512,12,64]{0,2,1:T(8,128)(2,1)S(1)} %bitcast.186, bf16[1024,12,64]{0,2,1:T(8,128)(2,1)S(1)} %bitcast.183), kind=kOutput, calls=%fused_computation.148 | convolution fusion | flops 824181760 | bytes 27549696 | tf_op jit(solution)/shard_map/sub | solution.py:464
  229.8 10.9 %fusion.51 = bf16[12,64,512]{2,1,0:T(8,128)(2,1)S(1)} fusion(bf16[1024,12,64]{0,2,1:T(8,128)(2,1)} %bitcast.191, f32[12,512,1024]{2,1,0:T(8,128)} %get-tuple-element.136, f32[12,512]{1,0:T(8,128)S(1)} %get-tuple-element.135), kind=kOutput, calls=%fused_computation.90 | convolution fusion | flops 818282496 | bytes 27549696 | tf_op jit(solution)/shard_map/hqk,khc->qhc/dot_general | solution.py:437
  240.8 0.9 fusion.79
  242.1 5.6 %fusion.22 = f32[4,768,512]{1,2,0:T(8,128)S(1)} fusion(bf16[4,2,768,768]{3,2,1,0:T(8,128)(2,1)} %get-tuple-element.93, f32[512,768]{1,0:T(8,128)S(1)} %get-tuple-element.138, f32[768]{0:T(1024)S(1)} %copy-done.32, f32[768]{0:T(1024)S(1)} %copy-done.28, f32[512]{0:T(512)S(1)} %add_rsqrt_fusion, f32[512]{0:T(512)S(1)} %broadcast_multiply_fusion.5), kind=kOutput, calls=%fused_computation.38 | convolution fusion | flops 2417885184 | bytes 12593152 | tf_op jit(solution)/shard_map/rd,sdh->srh/dot_general | solution.py:437
  247.8 6.5 %convert_reduce_fusion = (f32[4,768]{1,0:T(4,128)S(1)}, bf16[4,512,768]{2,1,0:T(8,128)(2,1)S(1)}) fusion(f32[4,768,512]{1,2,0:T(8,128)S(1)} %fusion.22, f32[4,768]{1,0:T(4,128)S(1)} %bitcast.200, bf16[512,768]{1,0:T(8,128)(2,1)S(1)} %copy-done.17, bf16[4,2,768,768]{3,2,1,0:T(8,128)(2,1)S(1)} %bitcast.204), kind=kOutput, calls=%fused_computation.30 | convolution fusion | flops 2452091904 | bytes 14966784 | tf_op jit(solution)/shard_map/rd,shd->srh/dot_general | solution.py:437
  254.3 3.0 fusion.45
  257.4 0.7 convert_reduce_fusion.3
  258.1 1.7 convolution_convert_fusion.1
  259.8 1.4 copy.39
  261.2 11.5 %fusion.39 = f32[1024,1,12,64]{0,3,2,1:T(8,128)} fusion(bf16[512,12,64]{0,2,1:T(8,128)(2,1)S(1)} %bitcast.198, f32[12,512,1024]{2,1,0:T(8,128)} %get-tuple-element.136, f32[12,512]{1,0:T(8,128)S(1)} %get-tuple-element.135), kind=kOutput, calls=%fused_computation.60 | convolution fusion | flops 817889280 | bytes 29122560 | tf_op jit(solution)/shard_map/hqk,qhc->khc/dot_general | solution.py:437
  272.8 17.4 %multiply_reduce_fusion = (f32[12,512]{1,0:T(8,128)S(1)}, f32[12,512,1024]{2,1,0:T(8,128)}) fusion(f32[12,512,1024]{2,1,0:T(8,128)} %get-tuple-element.136, f32[12,512]{1,0:T(8,128)S(1)} %get-tuple-element.135, bf16[512,12,64]{0,2,1:T(8,128)(2,1)S(1)} %bitcast.199, bf16[1024,12,64]{0,2,1:T(8,128)(2,1)} %bitcast.192), kind=kOutput, calls=%fused_computation.5 | convolution fusion | flops 824174592 | bytes 52740096 | tf_op jit(solution)/shard_map/qhc,khc->hqk/dot_general | solution.py:437
  290.1 16.3 %multiply_convert_fusion = bf16[12,512,1024]{2,1,0:T(8,128)(2,1)S(1)} fusion(f32[12,512,1024]{2,1,0:T(8,128)} %get-tuple-element.141, f32[12,512]{1,0:T(8,128)S(1)} %get-tuple-element.140, f32[12,512,1024]{2,1,0:T(8,128)} %get-tuple-element.136, f32[12,512]{1,0:T(8,128)S(1)} %get-tuple-element.135), kind=kLoop, calls=%fused_computation.4 | loop fusion | flops 25165824 | bytes 62963712 | tf_op jit(solution)/shard_map/convert_element_type | solution.py:493
  306.5 2.3 multiply_bitcast_fusion
  308.8 3.0 copy-done.2
  311.8 3.5 pad_maximum_fusion.1
  316.7 0.8 dynamic-update-slice.13
  317.4 17.1 %all-reduce.4 = f32[8]{0:T(128)S(1)} all-reduce(f32[8]{0:T(128)S(1)} %dynamic-update-slice.13), channel_id=1, replica_groups=mesh['dh'=1,'k'=4,'c'=2,'mp'=4] {'c','mp'}, use_global_device_ids=true, to_apply=%add.4 | all-reduce | flops 8 | bytes 64
  334.6 0.6 dynamic_slice.22
  335.8 1.8 convolution_convert_fusion
  337.6 7.5 %convert_bitcast_fusion.1 = bf16[4,1,768,768]{3,2,1,0:T(8,128)(2,1)} fusion(bf16[4,512,768]{2,1,0:T(8,128)(2,1)} %copy-done.38, f32[512,768]{1,0:T(8,128)} %copy-done.7, f32[768]{0:T(1024)S(1)} %copy-done.32, f32[768]{0:T(1024)S(1)} %copy-done.28, f32[512]{0:T(512)S(1)} %add_rsqrt_fusion, f32[512]{0:T(512)S(1)} %broadcast_multiply_fusion.5), kind=kOutput, calls=%fused_computation.46 | convolution fusion | flops 2420244480 | bytes 9447424 | tf_op jit(solution)/shard_map/rd,srh->sdh/dot_general | solution.py:437
  345.1 5.8 %convert_bitcast_fusion = bf16[4,1,768,768]{3,2,1,0:T(8,128)(2,1)} fusion(bf16[512,768]{1,0:T(8,128)(2,1)S(1)} %copy-done.18, f32[4,768,512]{1,2,0:T(8,128)S(1)} %bitcast.206, f32[4,768]{1,0:T(4,128)S(1)} %bitcast.201), kind=kOutput, calls=%fused_computation.45 | convolution fusion | flops 2434007040 | bytes 11808768 | tf_op jit(solution)/shard_map/srh,rd->shd/dot_general | solution.py:437
  350.9 8.2 %pad_maximum_fusion.gm_ref = bf16[4,2,768,768]{3,2,1,0:T(8,128)(2,1)} fusion(bf16[4,1,768,768]{3,2,1,0:T(8,128)(2,1)} %convert_bitcast_fusion, bf16[4,1,768,768]{3,2,1,0:T(8,128)(2,1)} %convert_bitcast_fusion.1), kind=kLoop, calls=%fused_computation.11 | loop fusion | flops 4718592 | bytes 18874368 | tf_op jit(solution)/shard_map/stack | solution.py:500
  359.1 9.1 %multiply_convert_fusion.1 = bf16[12,64,512]{2,1,0:T(8,128)(2,1)S(1)} fusion(bf16[1024,12,64]{0,2,1:T(8,128)(2,1)} %bitcast.184, bf16[12,512,1024]{2,1,0:T(8,128)(2,1)} %copy-done.2), kind=kOutput, calls=%fused_computation.76 | convolution fusion | flops 806092800 | bytes 14942208 | tf_op jit(solution)/shard_map/hqk,khc->qhc/dot_general | solution.py:437
  368.2 9.0 %fusion.43.oo_ref = bf16[512,768]{1,0:T(8,128)(2,1)} fusion(f32[512,768]{1,0:T(8,128)S(1)} %copy-done.8, bf16[4,2,768,768]{3,2,1,0:T(8,128)(2,1)} %get-tuple-element.93, f32[768]{0:T(1024)S(1)} %copy-done.33, f32[4,768,512]{1,2,0:T(8,128)} %copy-done.37, f32[4,768]{1,0:T(4,128)S(1)} %bitcast.202), kind=kOutput, calls=%fused_computation.64 | convolution fusion | flops 2432827392 | bytes 13384704 | tf_op jit(solution)/shard_map/srh,shd->rd/dot_general | solution.py:437
  377.3 2.2 convert_element_type.134
  379.5 4.6 multiply_reduce_fusion.2
  384.7 1.6 pad_maximum_fusion.3
  386.3 1.8 fusion.73
  389.3 4.2 fusion.70
  393.5 2.2 copy.64
  395.6 0.6 broadcast.191
  396.4 4.5 pad_maximum_fusion.2.ga_ref
  401.0 1.9 concatenate.18.small_ref
  402.9 129.8 %reduce_grads.1 = (bf16[4,192,768]{2,1,0:T(8,128)(2,1)}, bf16[2,768,768]{2,1,0:T(8,128)(2,1)}, f32[24,768]{1,0:T(8,128)}, f32[32,8,768]{2,1,0:T(8,128)}, f32[512,768]{1,0:T(8,128)}, /*index=5*/bf16[512,768]{1,0:T(8,128)(2,1)}) custom-call(bf16[4,4,192,768]{3,2,1,0:T(8,128)(2,1)} %pad_maximum_fusion.2.ga_ref, ...), custom_call_target="tpu_custom_call" | custom-call | tf_op jit(solution)/shard_map/reduce_grads/pallas_call | solution.py:411
  532.7 1.7 convert_reduce_fusion.4
  534.4 1.2 slice.205
  535.6 1.6 slice_reduce_fusion
  537.2 0.8 fusion.76
  538.1 1.8 bitcast_convert_fusion.2
  539.9 2.5 convert_bitcast_fusion.2
  542.4 0.6 dynamic-slice_reduce_fusion
  543.0 2.5 bitcast_convert_fusion
  546.2 3.0 fusion.60
  549.1 0.9 copy.72
  550.0 1.1 copy.73
  (134 shorter events, 5.0 us)
Async XLA Ops:
  7.2 5.5 copy-start
  7.2 207.2 %all-gather.2.cloned.1.call-start = ((), (), s32[]{:S(2)}) async-start(), calls=%async_computation.1 | async-start | bytes 4718592 | tf_op jit(solution)/shard_map/all_gather | solution.py:459
  13.3 2.8 copy-start.22
  16.1 181.2 %copy-start.29 = (f32[768]{0:T(1024)S(1)}, f32[768]{0:T(1024)}, u32[]{:S(2)}) copy-start(f32[768]{0:T(1024)} %param.38) | copy-start | bytes 9220
  16.1 181.2 %copy-start.34 = (f32[768]{0:T(1024)S(1)}, f32[768]{0:T(1024)}, u32[]{:S(2)}) copy-start(f32[768]{0:T(1024)} %param.39) | copy-start | bytes 9220
  194.8 7.0 %copy-start.24 = (f32[512]{0:T(512)}, f32[512]{0:T(512)S(1)}, u32[]{:S(2)}) copy-start(f32[512]{0:T(512)S(1)} %broadcast_multiply_fusion.6) | copy-start | bytes 6148
  196.3 5.5 copy-start.26
  201.8 1.4 copy-start.14
  204.4 172.8 %reduce-scatter.2.cloned.1.call-start = ((), (), s32[]{:S(2)}) async-start(), calls=%async_computation.2 | async-start | bytes 9437184 | tf_op jit(solution)/shard_map/reduce_scatter | solution.py:496
  209.0 20.7 %copy-start.10 = (bf16[512,4,1,3,64]{0,4,3,2,1:T(8,128)(2,1)}, bf16[512,4,1,3,64]{0,4,3,2,1:T(8,128)(2,1)S(1)}, u32[]{:S(2)}) copy-start(bf16[512,4,1,3,64]{0,4,3,2,1:T(8,128)(2,1)S(1)} %slice.229) | copy-start | bytes 2359300
  217.9 11.9 %copy-start.6 = (bf16[1024,4,1,3,64]{0,4,3,2,1:T(8,128)(2,1)}, bf16[1024,4,1,3,64]{0,4,3,2,1:T(8,128)(2,1)S(1)}, u32[]{:S(2)}) copy-start(bf16[1024,4,1,3,64]{0,4,3,2,1:T(8,128)(2,1)S(1)} %get-tuple-element.118) | copy-start | bytes 4718596
  229.8 10.9 %copy-start.3 = (bf16[512,768]{1,0:T(8,128)(2,1)S(1)}, bf16[512,768]{1,0:T(8,128)(2,1)}, u32[]{:S(2)}) copy-start(bf16[512,768]{1,0:T(8,128)(2,1)} %get-tuple-element.88) | copy-start | bytes 2359300
  229.8 11.0 %copy-start.16 = (bf16[4,1,192,768]{3,2,1,0:T(8,128)(2,1)S(1)}, bf16[4,1,192,768]{3,2,1,0:T(8,128)(2,1)}, u32[]{:S(2)}) copy-start(bf16[4,1,192,768]{3,2,1,0:T(8,128)(2,1)} %slice.198) | copy-start | bytes 3538948
  229.8 11.0 %copy-start.31 = (f32[768]{0:T(1024)S(1)}, f32[768]{0:T(1024)}, u32[]{:S(2)}) copy-start(f32[768]{0:T(1024)} %param.37) | copy-start | bytes 9220
  240.7 1.0 copy-start.19
  240.7 1.3 copy-start.28
  240.7 1.3 copy-start.32
  240.7 7.0 %slice-start = ((s8[9437184]{0:T(1024)(128)(4,1)}), s8[4194304]{0:T(1024)(128)(4,1)S(1)}, s32[]{:S(2)}) async-start(s8[9437184]{0:T(1024)(128)(4,1)} %bitcast.203), calls=%async_computation.3 | async-start | bytes 8388608
  241.7 15.6 %copy-start.7 = (f32[512,768]{1,0:T(8,128)}, f32[512,768]{1,0:T(8,128)S(1)}, u32[]{:S(2)}) copy-start(f32[512,768]{1,0:T(8,128)S(1)} %get-tuple-element.138) | copy-start | bytes 4718596
  242.1 5.7 %copy-start.17 = (bf16[512,768]{1,0:T(8,128)(2,1)S(1)}, bf16[512,768]{1,0:T(8,128)(2,1)}, u32[]{:S(2)}) copy-start(bf16[512,768]{1,0:T(8,128)(2,1)} %get-tuple-element.92) | copy-start | bytes 2359300
  242.1 5.7 %slice-start.1 = ((s8[9437184]{0:T(1024)(128)(4,1)}), s8[4194304]{0:T(1024)(128)(4,1)S(1)}, s32[]{:S(2)}) async-start(s8[9437184]{0:T(1024)(128)(4,1)} %bitcast.203), calls=%async_computation.4 | async-start | bytes 8388608
  242.1 5.7 %slice-start.2 = ((s8[9437184]{0:T(1024)(128)(4,1)}), s8[1048576]{0:T(1024)(128)(4,1)S(1)}, s32[]{:S(2)}) async-start(s8[9437184]{0:T(1024)(128)(4,1)} %bitcast.203), calls=%async_computation.5 | async-start | bytes 2097152
  247.7 6.6 %copy-start.37 = (f32[4,768,512]{1,2,0:T(8,128)}, f32[4,768,512]{1,2,0:T(8,128)S(1)}, u32[]{:S(2)}) copy-start(f32[4,768,512]{1,2,0:T(8,128)S(1)} %fusion.22) | copy-start | bytes 18874372
  254.3 3.0 copy-start.38
  290.1 16.4 %copy-start.11 = (bf16[512,4,1,3,64]{0,4,3,2,1:T(8,128)(2,1)S(1)}, bf16[512,4,1,3,64]{0,4,3,2,1:T(8,128)(2,1)}, u32[]{:S(2)}) copy-start(bf16[512,4,1,3,64]{0,4,3,2,1:T(8,128)(2,1)} %copy-done.10) | copy-start | bytes 2359300
  306.5 5.3 copy-start.2
  306.5 5.3 copy-start.12
  315.3 0.8 copy-start.36
  315.3 20.5 %copy-start.20 = (bf16[12,64,512]{2,1,0:T(8,128)(2,1)S(1)}, bf16[12,64,512]{2,1,0:T(8,128)(2,1)}, u32[]{:S(2)}) copy-start(bf16[12,64,512]{2,1,0:T(8,128)(2,1)} %copy-done.19) | copy-start | bytes 2359300
  335.8 9.3 %slice-start.3 = ((s8[6291456]{0:T(1024)(128)(4,1)}), s8[4194304]{0:T(1024)(128)(4,1)S(1)}, s32[]{:S(2)}) async-start(s8[6291456]{0:T(1024)(128)(4,1)} %bitcast.205), calls=%async_computation.6 | async-start | bytes 8388608
  337.6 7.5 %copy-start.18 = (bf16[512,768]{1,0:T(8,128)(2,1)S(1)}, bf16[512,768]{1,0:T(8,128)(2,1)}, u32[]{:S(2)}) copy-start(bf16[512,768]{1,0:T(8,128)(2,1)} %get-tuple-element.92) | copy-start | bytes 2359300
  337.6 7.5 %slice-start.4 = ((s8[6291456]{0:T(1024)(128)(4,1)}), s8[2097152]{0:T(1024)(128)(4,1)S(1)}, s32[]{:S(2)}) async-start(s8[6291456]{0:T(1024)(128)(4,1)} %bitcast.205), calls=%async_computation.7 | async-start | bytes 4194304
  359.1 9.1 %copy-start.8 = (f32[512,768]{1,0:T(8,128)S(1)}, f32[512,768]{1,0:T(8,128)}, u32[]{:S(2)}) copy-start(f32[512,768]{1,0:T(8,128)} %copy-done.7) | copy-start | bytes 4718596
  359.1 9.1 %copy-start.33 = (f32[768]{0:T(1024)S(1)}, f32[768]{0:T(1024)}, u32[]{:S(2)}) copy-start(f32[768]{0:T(1024)} %param.45) | copy-start | bytes 9220
  377.3 2.2 copy-start.25
  377.3 2.3 copy-start.27
  377.3 2.3 copy-start.30
  377.3 2.2 copy-start.4
  386.3 3.0 copy-start.5
  386.3 3.0 copy-start.35
  393.5 2.9 copy-start.9
  396.4 4.6 copy-start.23
  532.7 10.3 %copy-start.13 = (bf16[2,768,768]{2,1,0:T(8,128)(2,1)S(1)}, bf16[2,768,768]{2,1,0:T(8,128)(2,1)}, u32[]{:S(2)}) copy-start(bf16[2,768,768]{2,1,0:T(8,128)(2,1)} %get-tuple-element.99) | copy-start | bytes 7077892
  545.6 3.6 copy-start.21
  546.2 3.9 copy-start.15
  549.1 2.0 copy-start.1
Sparse Core Ops, SparseCore 0:
  204.6 9.8 all-gather.1
  315.5 15.6 reduce-scatter.1

commit v2 on v0

v2 whole, which is shorter than its diff:
```python
import functools

import jax
import jax.numpy as jnp
from jax import lax
from jax.experimental import pallas as pl
from jax.experimental.pallas import tpu as pltpu
from jax.sharding import Mesh, PartitionSpec as P

HEAD_DIM = 64
NSTEPS = 1000
L = 1024
EPSILON = 1e-05
HIGHEST = lax.Precision.HIGHEST
MESH = pl.DeviceIdType.MESH
BF = jnp.bfloat16
F32 = jnp.float32


def place():
    k = lax.axis_index("k")
    c = lax.axis_index("c")
    z = lax.axis_index("mp")
    return k, c, z


def flip(i, bit):
    if bit == 1:
        return i + 1 - 2 * lax.rem(i, 2)
    if bit == 2:
        return lax.rem(i + 2, 4)
    return 3 - i


def enter_barrier():
    k, c, z = place()
    sem = pltpu.get_barrier_semaphore()
    peers = [{"c": 1 - c}, {"k": flip(k, 1)}, {"k": flip(k, 2)}] + [{"mp": flip(z, r)} for r in (1, 2, 3)]
    peers.append({"c": 1 - c, "mp": flip(z, 1)})
    for peer in peers:
        pl.semaphore_signal(sem, inc=1, device_id=peer, device_id_type=MESH)
    pl.semaphore_wait(sem, len(peers))


def remote(src, dst, ss, rs, peer):
    return pltpu.make_async_remote_copy(src_ref=src, dst_ref=dst, send_sem=ss, recv_sem=rs, device_id=peer, device_id_type=MESH)


def cut(ref, lead, q, k, half, c):
    first, count = {None: (0, q), 0: (0, (q // 32) * 16 if q % 32 else q // 2), 1: ((q // 32) * 16 if q % 32 else q // 2, 0)}[half]
    if half == 1:
        count = q - first
    start = pl.multiple_of(k * q + first, 16)
    cols = pl.ds(pl.multiple_of(c * 384, 128), 384)
    return ref.at[lead + (slice(None), pl.ds(start, count), cols)]


def cols_of(ref, lead, c):
    return ref.at[lead + (slice(None), slice(None), pl.ds(pl.multiple_of(c * 384, 128), 384))]


def lane_mask(rows, j):
    lane = lax.broadcasted_iota(jnp.int32, (rows, 128), 1)
    return (lane < 64) if j == 0 else (lane >= 64)


def mm(a, b):
    return lax.dot_general(a, b, (((1,), (0,)), ((), ())), preferred_element_type=F32)


def mm_nt(a, b):
    return lax.dot_general(a, b, (((1,), (1,)), ((), ())), preferred_element_type=F32)


def norm_parts(values):
    center = values - jnp.mean(values, axis=-1, keepdims=True)
    inverse = lax.rsqrt(jnp.mean(center * center, axis=-1, keepdims=True) + EPSILON)
    return (center * inverse, inverse)


def norm_back(upstream, normal, inverse):
    return inverse * (
        upstream
        - jnp.mean(upstream, axis=-1, keepdims=True)
        - normal * jnp.mean(upstream * normal, axis=-1, keepdims=True)
    )


def col_sum(x):
    return jnp.sum(x, axis=0, keepdims=True)


def layer_kernel(qkv_ref, out_ref, in_ref, back_ref, bias_ref, tok_ref, grad_ref, row_ref, vec,
                 outa, outm, small_out, seq_out, ig_out, oo_out,
                 wa, wm, bias, tok, grad, row,
                 cra, crm, raa, rba, ram, rbm, bxa, bya, bxm, bym, za, zm, fa, fm, hyper, seq_buf,
                 gt, n1, q, kb, vb, att, lse, mid, acc, sg, n2, n2t, act, pg, br, dk_acc, dv_acc, dkt, dvt, dkr, dvr, igb,
                 local_sem, ssem, rsem, bsem, brem, wsem, wrem, kvs, kvr, dks, dkrs,
                 rss, rrs, fsem, frem, hsem, hrem, qsem, qrem, w2sem, w2rem):
    k, c, z = place()
    kx, ky, kd = flip(k, 1), flip(k, 2), flip(k, 3)
    nx, ny, nc = {"k": kx}, {"k": ky}, {"c": 1 - c}
    me = k * 8 + c * 4 + z
    every = slice(None)

    def start(cps):
        for cp in cps:
            cp.start()

    def got(cps):
        for cp in cps:
            cp.wait_recv()

    def sent(cps):
        for cp in cps:
            cp.wait_send()

    copies = [pltpu.make_async_copy(s, d, local_sem.at[i]) for i, (s, d) in enumerate([
        (qkv_ref, wa.at[0, pl.ds(0, 3)]),
        (out_ref, wa.at[0, 3]),
        (in_ref, wm.at[0, 0]),
        (back_ref, wm.at[0, 1]),
        (bias_ref, bias.at[0]),
    ])]
    start(copies)
    enter_barrier()
    stays = c == lax.rem(z, 2)
    moves = jnp.logical_not(stays)
    swap_peer = {"c": 1 - c, "mp": flip(z, 1)}

    def swap_start(remote_cps, local_cps):
        @pl.when(stays)
        def _():
            start(local_cps)

        @pl.when(moves)
        def _():
            start(remote_cps)

    def swap_wait(remote_cps, local_cps):
        @pl.when(stays)
        def _():
            for cp in local_cps:
                cp.wait()

        @pl.when(moves)
        def _():
            for cp in remote_cps:
                cp.wait()

    def swap_of(pairs, send, recv, first):
        return ([remote(s, d, send.at[i], recv.at[i], swap_peer) for i, (s, d) in enumerate(pairs)],
                [pltpu.make_async_copy(s, d, local_sem.at[first + i]) for i, (s, d) in enumerate(pairs)])

    swap_in = swap_of([(tok_ref, tok), (row_ref, row), (grad_ref, grad)], wsem, wrem, 5)
    for cp in copies[:2]:
        cp.wait()

    gchunks = [(wa, 48, 1), (wa, 48, 2), (wa, 48, 3), (wm, 192, 1), (wm, 192, 2), (wm, 192, 3)]
    ng = len(gchunks)

    def gsends(i):
        w, qr, r = gchunks[i]
        at = lambda slot, kk, half: cut(w, (slot,), qr, kk, half, c)
        return [
            [remote(at(0, k, None), at(r, k, None), ssem.at[i, 0], rsem.at[i, 0], {"mp": flip(z, r)})],
            [remote(at(r, k, None), at(r, k, None), ssem.at[i, 1], rsem.at[i, 1], nx),
             remote(at(r, k, None), at(r, k, None), ssem.at[i, 2], rsem.at[i, 2], ny)],
            [remote(at(r, ky, 0), at(r, ky, 0), ssem.at[i, 3], rsem.at[i, 3], nx),
             remote(at(r, kx, 1), at(r, kx, 1), ssem.at[i, 4], rsem.at[i, 4], ny)],
            [remote(cols_of(w, (r,), c), cols_of(w, (r,), c), ssem.at[i, 5], rsem.at[i, 5], nc)],
        ]

    def glands(i):
        w, qr, r = gchunks[i]
        at = lambda slot, kk, half: cut(w, (slot,), qr, kk, half, c)
        return [
            [(at(r, k, None), rsem.at[i, 0])],
            [(at(r, kx, None), rsem.at[i, 1]), (at(r, ky, None), rsem.at[i, 2])],
            [(at(r, kd, 0), rsem.at[i, 3]), (at(r, kd, 1), rsem.at[i, 4])],
            [(cols_of(w, (r,), 1 - c), rsem.at[i, 5])],
        ]

    g_sends = [gsends(i) for i in range(ng)]
    g_lands = [glands(i) for i in range(ng)]
    AHEAD = 2

    def gather_step(step):
        for stage in range(4):
            i = step - stage
            if 0 <= i < ng:
                for ref, sem in g_lands[i][stage]:
                    pltpu.make_async_copy(ref, ref, sem).wait()
                if stage == 0 and i + AHEAD < ng:
                    if i + AHEAD == 3:
                        for cp in copies[2:4]:
                            cp.wait()
                    start(g_sends[i + AHEAD][0])
                if stage < 3:
                    start(g_sends[i][stage + 1])

    small_cps = [remote(bias.at[0], bias.at[r], bsem.at[r - 1], brem.at[r - 1], {"mp": flip(z, r)}) for r in (1, 2, 3)]
    start(g_sends[0][0])
    copies[4].wait()
    start(small_cps)
    swap_start(*swap_in)
    start(g_sends[1][0])

    def ln_one():
        @pl.loop(0, 4)
        def _(i):
            r = pl.ds(pl.multiple_of(i * 128, 128), 128)
            hat, _inv = norm_parts(tok[r].astype(F32) + row[0:1].astype(F32))
            n1[r] = (hat * vec[0:1] + vec[1:2]).astype(BF)

    def transpose_into(dst, src, rows_n, cols0, cols_n):
        @pl.loop(0, rows_n // 128)
        def _(i):
            r = pl.ds(pl.multiple_of(i * 128, 128), 128)
            dst[pl.ds(cols0, cols_n), r] = jnp.transpose(src[r, pl.ds(cols0, cols_n)])

    def qkv_half(h):
        def one(p, dst, b):
            w = wa[2 * h:2 * h + 2, p].reshape(384, 768)

            @pl.loop(0, 2)
            def _(i):
                r = pl.ds(pl.multiple_of(i * 256, 256), 256)
                o = mm_nt(n1[r], w)
                if b is not None:
                    o = o + b
                dst[r, pl.ds(384 * h, 384)] = o.astype(BF)

        qb = bias[2 * h, 1:2, 0:384] + bias[2 * h + 1, 3:4, 0:384]
        vb_ = bias[2 * h, 2:3, 0:384] + bias[2 * h + 1, 4:5, 0:384]
        one(1, kb.at[c], None)
        one(2, vb.at[c], vb_)
        start(kv_cps[h])
        one(0, q, qb)

    half_cols = lambda ref, h: ref.at[every, pl.ds(384 * h, 384)]
    kv_cps = [[remote(half_cols(kb.at[c], h), half_cols(kb.at[c], h), kvs.at[h, 0], kvr.at[h, 0], nc),
               remote(half_cols(vb.at[c], h), half_cols(vb.at[c], h), kvs.at[h, 1], kvr.at[h, 1], nc)] for h in range(2)]

    def kv_wait(h):
        for j, b in enumerate((kb, vb)):
            pltpu.make_async_copy(half_cols(b.at[1 - c], h), half_cols(b.at[1 - c], h), kvr.at[h, j]).wait()

    QB = 256

    def attend(first, count):
        @pl.loop(0, count * (512 // QB))
        def _(n):
            t = first + n // (512 // QB)
            lanes = pl.ds(pl.multiple_of(t * 128, 128), 128)
            r = pl.ds(pl.multiple_of(lax.rem(n, 512 // QB) * QB, QB), QB)
            keys = kb[:, :, lanes].reshape(1024, 128)
            vals = vb[:, :, lanes].reshape(1024, 128)
            qs = q[r, lanes].astype(F32) * (HEAD_DIM ** -0.5)
            outs = []
            stats = lse[r]
            lane = lax.broadcasted_iota(jnp.int32, (QB, 128), 1)
            for j in range(2):
                s = mm_nt(jnp.where(lane_mask(QB, j), qs, 0.0).astype(BF), keys)
                peak = jnp.max(s, axis=-1, keepdims=True)
                e = jnp.exp(s - peak)
                total = jnp.sum(e, axis=-1, keepdims=True)
                o = mm(e.astype(BF), vals)
                outs.append(o / total)
                stats = jnp.where(lane == 2 * t + j, peak + jnp.log(total), stats)
            lse[r] = stats
            att[r, lanes] = jnp.where(lane_mask(QB, 0), outs[0], outs[1]).astype(BF)

    def out_and_norm():
        wo = wa[:, 3].reshape(768, 768)

        @pl.loop(0, 2)
        def _(i):
            r = pl.ds(pl.multiple_of(i * 256, 256), 256)
            m = (tok[r].astype(F32) + row[0:1].astype(F32)) + (mm(att[r], wo) + vec[4:5])
            mid[r] = m
            hat, _inv = norm_parts(m)
            n2[r] = (hat * vec[2:3] + vec[3:4]).astype(BF)

    C0 = 0.7978845608028654
    C1 = 0.044715

    def feed(r4):
        w_in = wm.at[r4, 0]
        w_back = wm.at[r4, 1]

        @pl.loop(0, 2)
        def _(i):
            r = pl.ds(pl.multiple_of(i * 256, 256), 256)
            u = mm(n2[r], w_in[...]) + bias[r4, 0:1]
            da = mm_nt(grad[r], w_back[...])
            uu = u * u
            th = jnp.tanh(u * (C0 + (C0 * C1) * uu))
            half = 0.5 * (1.0 + th)
            a = (u * half).astype(BF)
            slope = half + (0.5 * u) * (1.0 - th * th) * (C0 + (3.0 * C0 * C1) * uu)
            p = (da * slope).astype(BF)
            act[r] = a
            pg[r] = p
            f = mm(a, w_back[...])
            g2 = mm_nt(p, w_in[...])
            if r4 == 0:
                acc[r] = f
                sg[r] = g2
            else:
                acc[r] += f
                sg[r] += g2
        zr = flip2(z, r4)
        hyper[0, pl.ds(zr, 1)] = col_sum(pg[...].astype(F32))

    def feed_grads(r4):
        @pl.loop(0, 3)
        def _(i):
            r = pl.ds(pl.multiple_of(i * 256, 256), 256)
            wm[r4, 0, r] = mm(n2t[r], pg[...]).astype(BF)
            wm[r4, 1, r] = mm(gt[r], act[...]).astype(BF)

    def after_feed():
        zero = jnp.zeros((1, 768), F32)

        def body(i, sums):
            r = pl.ds(pl.multiple_of(i * 128, 128), 128)
            m = mid[r]
            n2[r] = (m + (acc[r] + vec[5:6])).astype(BF)
            hat, inv = norm_parts(m)
            g = sg[r]
            go = grad[r].astype(F32)
            mg = go + norm_back(g * vec[2:3], hat, inv)
            sg[r] = mg
            b = mg.astype(BF)
            br[r] = b
            return (sums[0] + col_sum(g * hat), sums[1] + col_sum(g), sums[2] + col_sum(b.astype(F32)), sums[3] + col_sum(go))

        sums = lax.fori_loop(0, 4, body, (zero,) * 4)
        hyper[0, 14:15] = sums[0]
        hyper[0, 15:16] = sums[1]
        hyper[0, 16:17] = sums[2]
        hyper[0, 17:18] = sums[3]

    def attended_back():
        wo = wa[:, 3].reshape(768, 768)

        @pl.loop(0, 2)
        def _(i):
            r = pl.ds(pl.multiple_of(i * 256, 256), 256)
            act[r] = mm_nt(br[r], wo).astype(BF)

    def out_grads():
        transpose_into(n2t, att, 512, 0, 768)
        for s in range(4):
            wa[s, 3] = mm(n2t[192 * s:192 * s + 192], br[...]).astype(BF)

    def attend_back(h):
        nq = 512 // QB

        @pl.loop(0, 3 * nq)
        def _(n):
            tt = n // nq
            t = 3 * h + tt
            i = lax.rem(n, nq)
            lanes = pl.ds(pl.multiple_of(t * 128, 128), 128)
            r = pl.ds(pl.multiple_of(i * QB, QB), QB)
            keys = kb[:, :, lanes].reshape(1024, 128)
            vals = vb[:, :, lanes].reshape(1024, 128)
            qs = q[r, lanes].astype(F32) * (HEAD_DIM ** -0.5)
            go = act[r, lanes].astype(F32)
            qs_t = jnp.transpose(qs).astype(BF)
            go_t = jnp.transpose(go).astype(BF)
            prod = go * att[r, lanes].astype(F32)
            stats = lse[r]
            lane = lax.broadcasted_iota(jnp.int32, (QB, 128), 1)
            dqs = []
            for j in range(2):
                mask = lane_mask(QB, j)
                s = mm_nt(jnp.where(mask, qs, 0.0).astype(BF), keys)
                le = jnp.sum(jnp.where(lane == 2 * t + j, stats, 0.0), axis=-1, keepdims=True)
                delta = jnp.sum(jnp.where(mask, prod, 0.0), axis=-1, keepdims=True)
                p = jnp.exp(s - le)
                dp = mm_nt(jnp.where(mask, go, 0.0).astype(BF), vals)
                ds = (p * (dp - delta)).astype(BF)
                dqs.append(mm(ds, keys))
                half = slice(64 * j, 64 * j + 64)
                dv = mm(go_t[half], p.astype(BF))
                dk = mm(qs_t[half], ds)

                @pl.when(i == 0)
                def _():
                    dv_acc[half] = dv
                    dk_acc[half] = dk

                @pl.when(i > 0)
                def _():
                    dv_acc[half] += dv
                    dk_acc[half] += dk
            dq = jnp.where(lane_mask(QB, 0), dqs[0], dqs[1]) * (HEAD_DIM ** -0.5)
            pg[r, lanes] = dq.astype(BF)

            @pl.when(i == nq - 1)
            def _():
                dkt[:, lanes_to_rows(t)] = jnp.stack([dk_acc[:, 0:512], dk_acc[:, 512:1024]]).astype(BF)
                dvt[:, lanes_to_rows(t)] = jnp.stack([dv_acc[:, 0:512], dv_acc[:, 512:1024]]).astype(BF)

        start(dkv_cps[h])

    lanes_to_rows = lambda t: pl.ds(pl.multiple_of(t * 128, 128), 128)
    rows_half = lambda ref, h: ref.at[pl.ds(384 * h, 384)]
    dkv_cps = [[remote(rows_half(dkt.at[1 - c], h), rows_half(dkr, h), dks.at[h, 0], dkrs.at[h, 0], nc),
                remote(rows_half(dvt.at[1 - c], h), rows_half(dvr, h), dks.at[h, 1], dkrs.at[h, 1], nc)] for h in range(2)]

    def qkv_back(h):
        got(dkv_cps[h])
        cols = pl.ds(384 * h, 384)
        transpose_into(gt, pg, 512, 384 * h, 384)

        @pl.loop(0, 3)
        def _(i):
            rr = pl.ds(pl.multiple_of(384 * h + i * 128, 128), 128)
            dkf = (dkt[c, rr].astype(F32) + dkr[rr].astype(F32)).astype(BF)
            dvf = (dvt[c, rr].astype(F32) + dvr[rr].astype(F32)).astype(BF)
            dkr[rr] = dkf
            dvr[rr] = dvf
            att[:, rr] = jnp.transpose(dkf)
            act[:, rr] = jnp.transpose(dvf)
        ws = [wa[2 * h:2 * h + 2, p].reshape(384, 768) for p in range(3)]

        @pl.loop(0, 2)
        def _(i):
            r = pl.ds(pl.multiple_of(i * 256, 256), 256)
            f = mm(pg[r, cols], ws[0]) + mm(att[r, cols], ws[1]) + mm(act[r, cols], ws[2])
            if h == 0:
                acc[r] = f
            else:
                acc[r] += f
        sums = (col_sum(pg[:, cols].astype(F32)), col_sum(act[:, cols].astype(F32)))
        lane = lax.broadcasted_iota(jnp.int32, (1, 384), 1)
        for j in range(2):
            zr = flip2(z, 2 * h + j)
            keep = (lane < 192) if j == 0 else (lane >= 192)
            for b, v in ((4, sums[0]), (8, sums[1])):
                hyper[0, pl.ds(b + zr, 1), 0:384] = jnp.where(keep, v, 0.0)
        for s in (2 * h, 2 * h + 1):
            rr = pl.ds(192 * s, 192)
            wa[s, 0] = mm(gt[rr], n1[...]).astype(BF)
            wa[s, 1] = mm(dkr[rr], n1[...]).astype(BF)
            wa[s, 2] = mm(dvr[rr], n1[...]).astype(BF)

    def last_norm():
        zero = jnp.zeros((1, 768), F32)

        def body(i, sums):
            r = pl.ds(pl.multiple_of(i * 128, 128), 128)
            hat, inv = norm_parts(tok[r].astype(F32) + row[0:1].astype(F32))
            g = acc[r]
            ig = sg[r] + norm_back(g * vec[0:1], hat, inv)
            igb[r] = ig.astype(BF)
            return (sums[0] + col_sum(g * hat), sums[1] + col_sum(g), sums[2] + col_sum(ig))

        sums = lax.fori_loop(0, 4, body, (zero,) * 3)
        hyper[0, 12:13] = sums[0]
        hyper[0, 13:14] = sums[1]
        seq_buf[pl.ds(me, 1), 0:1] = sums[2][None]
        step = row[1:2].astype(F32) * 32.0 + row[2:3].astype(F32)
        seq_buf[pl.ds(me, 1), 1:2] = step[None]

    chunks = [(wm, crm, r, 1, 192, ram, rbm, bxm, bym, zm) for r in range(4)]
    chunks += [(wa, cra, 2 * h, 2, 48, raa, rba, bxa, bya, za) for h in range(2)]
    mine = pl.ds(pl.multiple_of(c * 384, 128), 384)
    other = pl.ds(pl.multiple_of((1 - c) * 384, 128), 384)

    def rows(qr, kk, half):
        first = (qr // 32) * 16 if qr % 32 else qr // 2
        first, count = (0, qr) if half is None else ((0, first) if half == 0 else (first, qr - first))
        return pl.ds(pl.multiple_of(kk * qr + first, 16), count)

    def make(i):
        g, cr, s0, ns, qr, ra, rb, bx, by, zz = chunks[i]
        ss = pl.ds(s0, ns)
        return [
            [remote(g.at[ss, every, every, other], cr.at[ss], rss.at[i, 0], rrs.at[i, 0], nc)],
            [remote(g.at[ss, every, rows(qr, kd, 0), mine], ra.at[ss], rss.at[i, 1], rrs.at[i, 1], nx),
             remote(g.at[ss, every, rows(qr, kd, 1), mine], rb.at[ss], rss.at[i, 2], rrs.at[i, 2], ny)],
            [remote(g.at[ss, every, rows(qr, kx, None), mine], bx.at[ss], rss.at[i, 3], rrs.at[i, 3], nx),
             remote(g.at[ss, every, rows(qr, ky, None), mine], by.at[ss], rss.at[i, 4], rrs.at[i, 4], ny)],
            [remote(g.at[r, every, rows(qr, k, None), mine], zz.at[r - 1], rss.at[i, 4 + r], rrs.at[i, 4 + r], {"mp": flip(z, r)})
             for r in range(max(s0, 1), s0 + ns)],
        ]

    r_sends = [make(i) for i in range(len(chunks))]

    def add_into(dst, pieces):
        n, m = dst.shape[0], dst.shape[1]
        for a in range(n):
            for b in range(m):
                total = dst[a, b].astype(F32)
                for p in pieces:
                    total = total + p[a, b].astype(F32)
                dst[a, b] = total.astype(BF)

    def core_add(i):
        g, cr, s0, ns, qr, *_ = chunks[i]

        @pl.loop(0, 4)
        def _(j):
            r = pl.ds(pl.multiple_of(j * qr, 16), qr)
            add_into(g.at[pl.ds(s0, ns), :, r, mine], [cr.at[pl.ds(s0, ns), :, r]])

    def a_add(i):
        g, cr, s0, ns, qr, ra, rb, *_ = chunks[i]
        ss = pl.ds(s0, ns)
        add_into(g.at[ss, :, rows(qr, ky, 0), mine], [ra.at[ss]])
        add_into(g.at[ss, :, rows(qr, kx, 1), mine], [rb.at[ss]])

    def b_add(i):
        g, cr, s0, ns, qr, ra, rb, bx, by, zz = chunks[i]
        ss = pl.ds(s0, ns)
        add_into(g.at[ss, :, rows(qr, k, None), mine], [bx.at[ss], by.at[ss]])

    adds = [None, core_add, a_add, b_add]

    def reduce_stage(i, stage):
        if stage > 0:
            got(r_sends[i][stage - 1])
        if stage < 4:
            if stage > 0:
                adds[stage](i)
            start(r_sends[i][stage])

    finals = [(wm, zm, fm, 192, 0), (wa, za, fa, 48, 1)]

    def final_sends(j):
        g, zz, f, qr, _ = finals[j]
        at = lambda kk, half: f.at[:, rows(qr, kk, half), mine]
        return [
            [remote(at(k, None), at(k, None), fsem.at[j, 0], frem.at[j, 0], nx),
             remote(at(k, None), at(k, None), fsem.at[j, 1], frem.at[j, 1], ny)],
            [remote(at(ky, 0), at(ky, 0), fsem.at[j, 2], frem.at[j, 2], nx),
             remote(at(kx, 1), at(kx, 1), fsem.at[j, 3], frem.at[j, 3], ny)],
            [remote(f.at[:, :, mine], f.at[:, :, mine], fsem.at[j, 4], frem.at[j, 4], nc)],
        ]

    f_sends = [final_sends(j) for j in range(2)]

    def final_sum(j):
        g, zz, f, qr, _ = finals[j]
        for b in range(g.shape[1]):
            total = g[0, b, rows(qr, k, None), mine].astype(F32)
            for r in range(3):
                total = total + zz[r, b].astype(F32)
            f[b, rows(qr, k, None), mine] = total.astype(BF)
        start(f_sends[j][0])

    def final_stage(j, stage):
        got(f_sends[j][stage - 1])
        if stage < 3:
            start(f_sends[j][stage])

    hyper[0] = jnp.zeros(hyper.shape[1:], F32)
    seq_buf[pl.ds(me, 1)] = jnp.zeros((1, 8, 768), F32)
    lse[...] = jnp.zeros_like(lse)
    gather_step(0)
    swap_wait(*swap_in)
    ln_one()
    transpose_into(gt, grad, 512, 0, 768)
    gather_step(1)
    for cp in small_cps:
        cp.wait()
    gather_step(2)
    gather_step(3)
    qkv_half(0)
    gather_step(4)
    kv_wait(0)
    attend(0, 3)
    gather_step(5)
    qkv_half(1)
    gather_step(6)
    kv_wait(1)
    attend(3, 3)
    out_and_norm()
    transpose_into(n2t, n2, 512, 0, 768)
    gather_step(7)
    feed(0)
    gather_step(8)
    for i in range(ng):
        for stage in range(4):
            sent(g_sends[i][stage])
    feed_grads(0)
    reduce_stage(0, 0)
    feed(1)
    reduce_stage(0, 1)
    feed_grads(1)
    reduce_stage(1, 0)
    reduce_stage(0, 2)
    feed(2)
    reduce_stage(1, 1)
    reduce_stage(0, 3)
    feed_grads(2)
    reduce_stage(2, 0)
    reduce_stage(1, 2)
    feed(3)
    reduce_stage(0, 4)
    reduce_stage(2, 1)
    reduce_stage(1, 3)
    feed_grads(3)
    reduce_stage(3, 0)
    reduce_stage(2, 2)
    after_feed()
    swap_out = swap_of([(n2, oo_out)], w2sem, w2rem, 8)
    swap_start(*swap_out)
    reduce_stage(1, 4)
    reduce_stage(3, 1)
    reduce_stage(2, 3)
    attended_back()
    out_grads()
    reduce_stage(3, 2)
    attend_back(0)
    reduce_stage(2, 4)
    reduce_stage(3, 3)
    attend_back(1)
    sent(kv_cps[0] + kv_cps[1])
    reduce_stage(3, 4)
    final_sum(0)
    qkv_back(0)
    reduce_stage(4, 0)
    final_stage(0, 1)
    qkv_back(1)
    reduce_stage(5, 0)
    final_stage(0, 2)
    reduce_stage(4, 1)
    last_norm()
    swap_ig = ([remote(igb, ig_out, w2sem.at[1], w2rem.at[1], swap_peer)], [pltpu.make_async_copy(igb, ig_out, local_sem.at[9])])
    swap_start(*swap_ig)
    reduce_stage(5, 1)
    final_stage(0, 3)
    out_m = pltpu.make_async_copy(fm, outm, local_sem.at[10])
    out_m.start()
    peers = [nc, nx, ny, {"mp": flip(z, 1)}, {"mp": flip(z, 2)}]
    hops = [remote(hyper.at[2 * t], hyper.at[2 * t + 1], hsem.at[t], hrem.at[t], peer) for t, peer in enumerate(peers)]

    def hop(t):
        got([hops[t]])
        hyper[2 * t + 2] = hyper[2 * t] + hyper[2 * t + 1]
        if t < 4:
            start([hops[t + 1]])

    mine_seq = seq_buf.at[pl.ds(me, 1)]
    zq = lambda kk, cc, zz_: seq_buf.at[pl.ds(kk * 8 + cc * 4 + zz_, 1)]
    line = lambda kk, cc: seq_buf.at[pl.ds(kk * 8 + cc * 4, 4)]
    chip = lambda kk: seq_buf.at[pl.ds(kk * 8, 8)]
    q_sends = [
        [remote(mine_seq, mine_seq, qsem.at[r - 1], qrem.at[r - 1], {"mp": flip(z, r)}) for r in (1, 2, 3)],
        [remote(line(k, c), line(k, c), qsem.at[3], qrem.at[3], nc)],
        [remote(chip(k), chip(k), qsem.at[4], qrem.at[4], nx), remote(chip(k), chip(k), qsem.at[5], qrem.at[5], ny)],
        [remote(chip(ky), chip(ky), qsem.at[6], qrem.at[6], nx)],
    ]
    start(q_sends[0])
    start([hops[0]])
    reduce_stage(4, 2)
    hop(0)
    reduce_stage(5, 2)
    got(q_sends[0])
    start(q_sends[1])
    hop(1)
    reduce_stage(4, 3)
    got(q_sends[1])
    start(q_sends[2])
    reduce_stage(5, 3)
    hop(2)
    got(q_sends[2])
    start(q_sends[3])
    reduce_stage(4, 4)
    reduce_stage(5, 4)
    final_sum(1)
    hop(3)
    final_stage(1, 1)
    hop(4)
    small_cp = pltpu.make_async_copy(hyper.at[10], small_out, local_sem.at[11])
    small_cp.start()
    final_stage(1, 2)
    got(q_sends[3])
    seq_cp = pltpu.make_async_copy(seq_buf, seq_out, local_sem.at[12])
    seq_cp.start()
    final_stage(1, 3)
    out_a = pltpu.make_async_copy(fa, outa, local_sem.at[13])
    out_a.start()
    for st in r_sends + f_sends + q_sends_list(q_sends):
        for cps in st:
            sent(cps)
    sent(hops)
    sent(dkv_cps[0] + dkv_cps[1])
    swap_wait(*swap_out)
    swap_wait(*swap_ig)
    for cp in (out_m, small_cp, seq_cp, out_a):
        cp.wait()


def q_sends_list(q_sends):
    return [q_sends]


def flip2(z, r):
    return z if r == 0 else flip(z, r)


def layer(qkv, out, win, back, bias, tok, grad, row, vec):
    hbm = pl.BlockSpec(memory_space=pl.ANY)
    dma = pltpu.SemaphoreType.DMA
    vm = pltpu.VMEM
    shapes = (
        jax.ShapeDtypeStruct((4, 192, 768), BF),
        jax.ShapeDtypeStruct((2, 768, 768), BF),
        jax.ShapeDtypeStruct((24, 768), F32),
        jax.ShapeDtypeStruct((32, 8, 768), F32),
        jax.ShapeDtypeStruct((512, 768), BF),
        jax.ShapeDtypeStruct((512, 768), BF),
    )
    rows16 = vm((512, 768), BF)
    rows32 = vm((512, 768), F32)
    scratch = [
        vm((4, 4, 192, 768), BF), vm((4, 2, 768, 768), BF), vm((4, 8, 768), F32), rows16, rows16, vm((16, 768), BF),
        vm((4, 4, 192, 384), BF), vm((4, 2, 768, 384), BF),
        vm((4, 4, 16, 384), BF), vm((4, 4, 32, 384), BF), vm((4, 2, 96, 384), BF), vm((4, 2, 96, 384), BF),
        vm((4, 4, 48, 384), BF), vm((4, 4, 48, 384), BF), vm((4, 2, 192, 384), BF), vm((4, 2, 192, 384), BF),
        vm((3, 4, 48, 384), BF), vm((3, 2, 192, 384), BF), vm((4, 192, 768), BF), vm((2, 768, 768), BF),
        vm((11, 24, 768), F32), vm((32, 8, 768), F32),
        vm((768, 512), BF), rows16, rows16, vm((2, 512, 768), BF), vm((2, 512, 768), BF), rows16, vm((512, 128), F32),
        rows32, rows32, rows32, rows16, vm((768, 512), BF), rows16, rows16, rows16,
        vm((128, 1024), F32), vm((128, 1024), F32), vm((2, 768, 512), BF), vm((2, 768, 512), BF), vm((768, 512), BF), vm((768, 512), BF),
        rows16,
        dma((14,)), dma((6, 6)), dma((6, 6)), dma((3,)), dma((3,)), dma((3,)), dma((3,)),
        dma((2, 2)), dma((2, 2)), dma((2, 2)), dma((2, 2)),
        dma((6, 8)), dma((6, 8)), dma((2, 5)), dma((2, 5)), dma((5,)), dma((5,)), dma((7,)), dma((7,)), dma((2,)), dma((2,)),
    ]
    return pl.pallas_call(
        layer_kernel,
        out_shape=shapes,
        in_specs=[hbm] * 8 + [pl.BlockSpec(memory_space=pltpu.VMEM)],
        out_specs=[hbm] * 6,
        scratch_shapes=scratch,
        compiler_params=pltpu.CompilerParams(collective_id=0, has_side_effects=True, vmem_limit_bytes=63 << 20),
        name="layer",
    )(qkv, out, win, back, bias, tok, grad, row, vec)


def shards(tokens, timesteps, masked, cotangent, step_table, qkv_weight, qv_bias, out_weight, out_bias,
           first_gain, first_shift, second_gain, second_shift, in_weight, in_bias, back_weight, back_bias):
    z = lax.axis_index("mp")
    step = lax.dynamic_index_in_dim(timesteps, z // 2, keepdims=False)
    row = lax.dynamic_slice_in_dim(step_table, step, 1, axis=0)
    parts = jnp.stack([step // 32, step % 32]).astype(BF)
    row16 = jnp.concatenate([row, jnp.broadcast_to(parts[:, None], (2, 768)), jnp.zeros((13, 768), BF)])
    grad_low = cotangent * masked.astype(BF)[:, None]
    low_lanes = jnp.pad(qv_bias, ((0, 0), (0, 576)))
    high_lanes = jnp.pad(qv_bias, ((0, 0), (192, 384)))
    bias = jnp.concatenate([in_bias.astype(F32)[None], low_lanes, high_lanes, jnp.zeros((3, 768), F32)])
    vec = jnp.stack([first_gain, first_shift, second_gain, second_shift, out_bias, back_bias, out_bias, out_bias])
    outa, outm, small, seqs, input_grad, output = layer(
        qkv_weight.transpose(1, 2, 0), out_weight, in_weight, back_weight, bias, tokens, grad_low, row16, vec)
    onehot = (jnp.arange(NSTEPS, dtype=jnp.int32)[:, None] == seqs[:, 1, 0].astype(jnp.int32)[None, :]).astype(F32)
    table = jnp.dot(onehot, seqs[:, 0], precision=HIGHEST)
    qkv_g = outa[:3].astype(F32)
    out_g = outa[3].astype(F32)
    in_g = outm[0].astype(F32)
    back_g = outm[1].astype(F32).T
    if lax.axis_size("dh") > 1:
        table, qkv_g, out_g, in_g, back_g, small = lax.psum((table, qkv_g, out_g, in_g, back_g, small), "dh")
    own = lambda first: lax.dynamic_index_in_dim(small[first:first + 4], z, keepdims=False)
    qv_g = jnp.stack([own(4)[:192] + own(4)[192:384], own(8)[:192] + own(8)[192:384]])
    return (output, input_grad.astype(F32), table, qkv_g.transpose(2, 0, 1), qv_g, out_g, small[16],
            small[12], small[13], small[14], small[15], in_g, own(0), back_g, small[17])


def solution(mesh):
    n_dp, n_mp = mesh.devices.shape
    fine = Mesh(mesh.devices.reshape(n_dp // 8, 4, 2, n_mp), ("dh", "k", "c", "mp"))
    dp = ("dh", "k", "c")
    rows = dp + ("mp",)
    in_specs = (P(rows, None), P(dp), P(rows), P(rows, None), P(), P(None, None, "mp"), P(None, "mp"), P("mp", None),
                P(), P(), P(), P(), P(), P(None, "mp"), P("mp"), P("mp", None), P())
    out_specs = (P(rows, None), P(rows, None), P(), P(None, None, "mp"), P(None, "mp"), P("mp", None), P(), P(), P(), P(), P(),
                 P(None, "mp"), P("mp"), P("mp", None), P())
    return jax.shard_map(shards, mesh=fine, in_specs=in_specs, out_specs=out_specs, check_vma=False)
```

time: 1150 us -> 253 us (0.22)
  waiting for transfers between devices: 857 us -> 0 us
  Pallas kernels: 0 us -> 215 us
  matrix products: 106 us -> 2.99 us
  blocking collectives: 56.6 us -> 0 us
  local copies, waits for them, and re-layouts: 65.9 us -> 13.4 us
  other arithmetic: 37 us -> 13.4 us
    reduce_scatter x4 -> x0, waiting for transfers between devices: 412 us -> none  [the longest x1 111 us: shards(): lax.psum_scatter(jnp.dot(active, back_weight, preferred_element_type=jnp....]
    all_gather x4 -> x0, waiting for transfers between devices: 250 us -> none  [the longest x1 66.1 us: shards(): first_all = lax.all_gather(normed_one, 'mp', axis=0, tiled=True)]
    pallas_call x0 -> x1, Pallas kernels: none -> 215 us  [layer(): pl.pallas_call(layer_kernel, out_shape=shapes, in_specs=[hbm] * 8 + [pl.B...]
    psum x2 -> x0, waiting for transfers between devices: 195 us -> none  [the longest x1 143 us: shards(): lax.psum((first_gain_grad, first_shift_grad, second_gain_grad, second_shi...]
    dot_general x41 -> x1, matrix products: 99.3 us -> 2.99 us  [shards(): table = jnp.dot(onehot, seqs[:, 0], precision=HIGHEST)]
    psum x2 -> x0, blocking collectives: 56.6 us -> none  [the longest x1 41.2 us: shards(): lax.psum((first_gain_grad, first_shift_grad, second_gain_grad, second_shi...]
    reduce_sum x12 -> x0, other arithmetic: 21.4 us -> none  [the longest x4 5.22 us: attend_block(): totals = jnp.sum(exponent, axis=-1, keepdims=True)]
    while x43 -> x0, local copies, waits for them, and re-layouts: 19.4 us -> none
  transfers between devices with their start and end apart: 10 -> 0, of which waited for: 10 -> 0; matrix products, arithmetic and copies ran while one was open for 4% -> 0% of each run, Pallas kernels for 0% -> 0%
where the time goes in v2:
time: 253 us; the launch traced here: 250 us
  Pallas kernels  215 us (85%)
  local copies, waits for them, and re-layouts  13.4 us (5%)
  other arithmetic  13.4 us (5%)
  between operations  4.64 us (2%)
  matrix products  2.99 us (1%)
    pallas_call x1, Pallas kernels, layer(): pl.pallas_call(layer_kernel, out_shape=shapes, in_specs=[hbm] * 8 + [pl.B...  215 us

profile of v2, /device:TPU:0, one launch (start us, length us, event | category | flops | bytes accessed | tf_op | source)
XLA Modules:
  0.0 249.5 jit_solution(14302542558519844031)
XLA Ops:
  0.6 0.0 copy-start.3
  0.7 0.0 copy-start.4
  0.7 1.2 dynamic_slice.19
  4.5 0.1 pad_maximum_fusion.1
  5.9 0.7 constant_dynamic-slice_fusion
  6.6 0.1 pad.14.clone
  6.7 0.7 maximum_maximum_fusion.row_ref
  7.4 0.7 convert_element_type.44
  8.1 2.1 broadcast_multiply_fusion.grad_ref
  10.2 0.7 stack.40
  10.9 0.7 stack.41
  11.6 0.7 stack.42
  12.3 0.7 stack.43
  13.0 0.7 stack.44
  13.7 0.7 stack.45
  14.4 0.6 stack.46.vec
  15.0 0.0 copy-done.3
  15.0 0.1 pad.20.clone
  15.1 0.0 copy-done.4
  15.1 0.7 fusion.4.bias_ref
  15.8 215.2 %layer.1 = (bf16[4,192,768]{2,1,0:T(8,128)(2,1)}, bf16[2,768,768]{2,1,0:T(8,128)(2,1)}, f32[24,768]{1,0:T(8,128)}, f32[32,8,768]{2,1,0:T(8,128)}, bf16[512,768]{1,0:T(8,128)(2,1)}, /*index=5*/bf16[512,768]{1,0:T(8,128)(2,1)}) custom-call(bf16[3,192,768]{2,1,0:T(8,128)(2,1)} %bitcast.20, bf16[192,768]{1,0:T(8,128)(2,1)} %out_ref.1, bf16[768,768]{1,0:T(8,128)(2,1)} %in_ref.1, ...), custom_call_target="tpu_custom_call" | custom-call | tf_op jit(solution)/shard_map/layer/pallas_call | solution.py:738
  231.0 0.8 fusion.7
  231.8 0.1 dynamic-slice_add_fusion
  231.9 0.6 pad_maximum_fusion
  232.5 3.4 %convert_bitcast_fusion = (f32[768,768]{0,1:T(8,128)S(1)}, f32[768,768]{1,0:T(8,128)}) fusion(bf16[2,768,768]{2,1,0:T(8,128)(2,1)} %get-tuple-element.26), kind=kLoop, calls=%fused_computation | loop fusion | flops 1179648 | bytes 7077888 | tf_op jit(solution)/shard_map/transpose | solution.py:768
  235.9 1.9 copy.33
  237.8 0.0 copy-start
  237.8 1.6 slice_reduce_fusion
  239.5 1.2 slice.64
  240.6 1.6 convert_reduce_fusion
  242.2 3.0 %fusion = f32[1000,768]{1,0:T(8,128)} fusion(s32[32]{0:T(128)S(1)} %convert_reduce_fusion, f32[32,1,768]{2,1,0:T(1,128)S(1)} %slice.64), kind=kOutput, calls=%fused_computation.4 | convolution fusion | flops 294944000 | bytes 3170432 | tf_op jit(solution)/shard_map/dot_general | solution.py:764
  245.2 0.0 copy-start.2
  245.2 0.0 copy-done
  245.2 1.4 convert_bitcast_fusion.1
  246.5 0.0 copy-start.1
  246.6 0.0 copy-done.2
  246.6 1.3 convert_element_type.45
  247.8 0.9 bitcast_convert_fusion.1
  248.7 0.0 copy-done.1
  248.7 0.9 copy.40
  (3 shorter events, 0.0 us)
Async XLA Ops:
  0.6 14.4 %copy-start.3 = (bf16[768]{0:T(1024)(128)(2,1)S(1)}, bf16[768]{0:T(1024)(128)(2,1)}, u32[]{:S(2)}) copy-start(bf16[768]{0:T(1024)(128)(2,1)} %param.31) | copy-start | bytes 4612
  0.7 14.5 %copy-start.4 = (f32[2,192]{1,0:T(2,128)S(1)}, f32[2,192]{1,0:T(2,128)}, u32[]{:S(2)}) copy-start(f32[2,192]{1,0:T(2,128)} %param.23) | copy-start | bytes 4612
  237.8 7.4 %copy-start = (bf16[4,192,768]{2,1,0:T(8,128)(2,1)S(1)}, bf16[4,192,768]{2,1,0:T(8,128)(2,1)}, u32[]{:S(2)}) copy-start(bf16[4,192,768]{2,1,0:T(8,128)(2,1)} %get-tuple-element.24) | copy-start | bytes 3538948
  245.2 1.4 copy-start.2
  246.5 2.1 copy-start.1
